TPU v7x, 128 devices: a whole 4x4x4 slice. The times are simulated.
128 devices in a mesh: band: 16 (over z, y), slab: 8 (over x, core).
Axes of the slice: x: 4, y: 4, z: 4, core: 2. Of those that a mesh axis runs over, the one named last changes fastest.
Arguments:
- orbitals: float32 [64, 96, 18432], P('band', 'slab'), may hold values from -0.07 to 0.07
- potential: float32 [96, 9216], P('slab'), may hold values from -6 to 2
Outputs:
- evolved: float32 [64, 96, 18432], P('band', 'slab')
- hartree: float32 [96, 9216], P('slab')
All inputs are finite; a program needn't handle non-finite values.
Results may differ from a plain program's by a relative error of at most 0.0003.
Values sent between devices are 32-bit elements; how exact they have to be, the bound alone decides.
A program may use at most 128 MiB of HBM per device.

v0:
```python
import functools
import math

import jax
import jax.numpy as jnp
import ml_dtypes
import numpy as np
from jax import lax
from jax.experimental import pallas as pl
from jax.experimental.pallas import tpu as pltpu
from jax.sharding import PartitionSpec as P

GRID = 96
TIME_STEP = 0.1
MESH = pl.DeviceIdType.MESH
SLABS = 8
GROUPS = 16
BANDS = 4
OWN = GRID // SLABS
LINE = OWN * GRID
TILES = LINE // 128
BLOCK = TILES * 2 * OWN
BAND = SLABS * BLOCK
PAIRS = GRID // 2
SHARE = GRID // GROUPS
F32 = jnp.float32
BF16 = jnp.bfloat16


def half_step_factor():
    n = np.arange(GRID)
    m = (n + GRID // 2) % GRID - GRID // 2
    k = 2.0 * math.pi / GRID * m
    phase = np.exp(-1j * k * k * TIME_STEP / 4)
    diff = (n[:, None] - n[None, :]) % GRID
    line = np.fft.ifft(phase)
    full = line[diff]
    out = np.zeros((2, GRID, 2, GRID))
    out[0, :, 0] = full.real
    out[0, :, 1] = -full.imag
    out[1, :, 0] = full.imag
    out[1, :, 1] = full.real
    return out


def real_basis():
    n = np.arange(GRID)
    rows, ksq = [np.full(GRID, 1.0 / math.sqrt(GRID))], [0.0]
    for m in range(1, GRID // 2):
        angle = 2.0 * math.pi * ((m * n) % GRID) / GRID
        rows += [np.cos(angle) * math.sqrt(2.0 / GRID), np.sin(angle) * math.sqrt(2.0 / GRID)]
        ksq += [(2.0 * math.pi * m / GRID) ** 2] * 2
    rows.append(np.where(n % 2 == 0, 1.0, -1.0) / math.sqrt(GRID))
    ksq.append(math.pi**2)
    return np.stack(rows), np.array(ksq)


def split(matrix):
    high = matrix.astype(np.float32).astype(ml_dtypes.bfloat16)
    low = (matrix - high.astype(np.float64)).astype(ml_dtypes.bfloat16)
    return np.stack([high, low])


@functools.lru_cache(maxsize=None)
def tables():
    g = half_step_factor()
    t = {}
    into = g.transpose(2, 3, 0, 1)
    padded = np.zeros((2, GRID, 2, 128))
    padded[..., :GRID] = into
    padded = padded.reshape(2 * GRID, 256)
    za = np.zeros((2, 256, 256))
    za[0, :192] = padded
    za[1, 64:] = padded
    t["z_in"] = np.stack([split(za[0]), split(za[1])]).reshape(4 * 256, 256)
    rows = np.zeros((2, 128, 2, GRID))
    rows[:, :GRID] = into
    rows = rows.reshape(256, 2 * GRID)
    zb = np.zeros((2, 256, 256))
    zb[0, :, :192] = rows
    zb[1, :, 64:] = rows
    t["z_out"] = np.stack([split(zb[0]), split(zb[1])]).reshape(4 * 256, 256)
    j, s, a = np.meshgrid(np.arange(4), np.arange(SLABS), np.arange(3), indexing="ij")
    wire_y = 12 * s + 4 * a + j
    pair_y = 2 * np.arange(PAIRS)[None, :] + np.arange(2)[:, None]
    ky = g[:, wire_y][:, :, :, :, :, pair_y]
    t["y_in"] = split(ky.transpose(1, 0, 2, 3, 5, 4, 6).reshape(192, 192)).reshape(384, 192)
    ky = g[:, pair_y][:, :, :, :, wire_y]
    t["y_out"] = split(ky.transpose(1, 0, 2, 4, 3, 5, 6).reshape(192, 192)).reshape(384, 192)
    kx = g.reshape(2, GRID, 2, SLABS, OWN)
    t["x_in"] = split(kx.transpose(0, 1, 3, 2, 4).reshape(192, 192)).reshape(384, 192)
    kx = g.reshape(2, SLABS, OWN, 2, GRID)
    t["x_out"] = split(kx.transpose(1, 0, 2, 3, 4).reshape(192, 192)).reshape(384, 192)
    q, ksq = real_basis()
    qx = np.zeros((GROUPS, 8, GRID))
    qx[:, :SHARE] = q.reshape(GROUPS, SHARE, GRID)
    qx = qx.reshape(128, GRID)
    t["qx"] = split(qx).reshape(256, GRID)
    t["qxt"] = split(qx.T).reshape(192, 128)
    qz = np.zeros((128, 128))
    qz[:GRID, :GRID] = q.T
    t["qz"] = split(qz).reshape(256, 128)
    t["qzt"] = split(qz.T).reshape(256, 128)
    aj_s = 12 * np.arange(SLABS)[None, :] + np.arange(OWN)[:, None]
    t["qy"] = split(q[:, aj_s.reshape(-1)]).reshape(192, GRID)
    qyt = np.zeros((SLABS, 16, GRID))
    qyt[:, :OWN] = q.T.reshape(SLABS, OWN, GRID)
    t["qyt"] = split(qyt).transpose(1, 0, 2, 3).reshape(SLABS, 32, GRID)
    kxz = np.ones((GROUPS, 8, 128))
    kxz[:, :SHARE, :GRID] = ksq.reshape(GROUPS, SHARE)[:, :, None] + ksq[None, None, :]
    t["kxz"] = kxz.astype(np.float32)
    t["ky2"] = np.broadcast_to(ksq[:, None], (GRID, 128)).astype(np.float32)
    return t


NAMES = ("z_in", "z_out", "y_in", "y_out", "x_in", "x_out", "qx", "qxt", "qz", "qzt", "qy", "qyt", "kxz", "ky2")


def halves(x):
    high = x.astype(BF16)
    return high, (x - high.astype(F32)).astype(BF16)


def dot(a, b):
    return jnp.dot(a, b, preferred_element_type=F32)


def times(x, high, low):
    xh, xl = halves(x)
    return dot(xh, high) + (dot(xl, high) + dot(xh, low))


def left(high, low, x):
    xh, xl = halves(x)
    return dot(high, xh) + (dot(high, xl) + dot(low, xh))


def sin_cos(t):
    n = jnp.round(t * (2.0 / math.pi))
    r = t - n * 1.5703125
    r = r - n * 4.8375129699707031e-4
    r = r - n * 7.5495649e-08
    r2 = r * r
    sine = r + r * r2 * (-1.6666654611e-1 + r2 * (8.3321608736e-3 + r2 * -1.9515295891e-4))
    cosine = 1.0 - 0.5 * r2 + r2 * r2 * (4.166664568298827e-2 + r2 * (-1.388731625493765e-3 + r2 * 2.443315711809948e-5))
    quarter = n.astype(jnp.int32) & 3
    odd = (quarter & 1) == 1
    s = jnp.where(odd, cosine, sine)
    c = jnp.where(odd, sine, cosine)
    s = jnp.where(quarter >= 2, -s, s)
    c = jnp.where((quarter == 1) | (quarter == 2), -c, c)
    return s, c


def lane_of(shape):
    return lax.broadcasted_iota(jnp.int32, shape, len(shape) - 1)


def packed(parts):
    lane = lane_of(parts[0].shape)
    r1 = pltpu.roll(parts[1], 96, 1)
    r2 = pltpu.roll(parts[2], 64, 1)
    r3 = pltpu.roll(parts[3], 32, 1)
    return (
        jnp.where(lane < 96, parts[0], r1),
        jnp.where(lane < 64, r1, r2),
        jnp.where(lane < 32, r2, r3),
    )


def unpacked(tiles):
    lane = lane_of(tiles[0].shape)
    return (
        tiles[0],
        pltpu.roll(jnp.where(lane < 64, tiles[1], tiles[0]), 32, 1),
        pltpu.roll(jnp.where(lane < 32, tiles[2], tiles[1]), 64, 1),
        pltpu.roll(tiles[2], 96, 1),
    )


def kernel(orb, pot, z_in, z_out, y_in, y_out, x_in, x_out, qx, qxt, qz, qzt, qy, qyt, kxz, ky2,
           ev, har,
           ib, plane, wire, lines, moved, back, home, ob, dens, dq, part, share, modes, whole, zt, green, hq, hart,
           vb, vl, cosb, sinb, hs,
           in_sem, out_sem, pot_s, pot_r, w_s, w_r, b_s, b_r, rs_s, rs_r, ag_s, ag_r, hq_s, hq_r, h_s, h_r, own_sem):
    me = lax.axis_index("slab")
    grp = lax.axis_index("band")
    slab_peers = [(d, lax.rem(me + d, SLABS)) for d in range(1, SLABS)]
    band_peers = [(d, lax.rem(grp + d, GROUPS)) for d in range(1, GROUPS)]

    barrier = pltpu.get_barrier_semaphore()
    for _, q in slab_peers:
        pl.semaphore_signal(barrier, inc=1, device_id={"slab": q}, device_id_type=MESH)
    for _, q in band_peers:
        pl.semaphore_signal(barrier, inc=1, device_id={"band": q}, device_id_type=MESH)

    def load(b):
        return pltpu.make_async_copy(orb.at[b], ib.at[b], in_sem.at[b])

    for b in range(BANDS):
        load(b).start()

    def slab_copy(src, dst, s, r, q):
        return pltpu.make_async_remote_copy(src, dst, s, r, device_id={"slab": q}, device_id_type=MESH)

    def band_copy(src, dst, s, r, q):
        return pltpu.make_async_remote_copy(src, dst, s, r, device_id={"band": q}, device_id_type=MESH)

    def first(b, carry):
        load(b).wait()

        rest = jnp.zeros((16 - OWN, 256), F32)

        def kz(chunk, carry):
            start = pl.multiple_of(chunk * (8 * 384), 128)
            for j in range(2):
                x = jnp.concatenate(
                    [piece for i in range(8) for piece in (ib[b, :, pl.ds(start + 384 * i + 128 * j, 256)], rest)], 0
                )
                r = times(x, z_in[pl.ds(512 * j, 256)], z_in[pl.ds(512 * j + 256, 256)])
                for c in range(2):
                    row = pl.multiple_of(768 * (2 * j + c) + chunk * 128, 128)
                    plane[pl.ds(row, 128)] = r[:, 128 * c : 128 * c + 128]
            return carry

        lax.fori_loop(0, 6, kz, 0)

        def ky(pair, carry):
            cols = []
            for i in range(2):
                x = 2 * pair + i
                cols.append(
                    jnp.concatenate([plane[pl.ds(768 * k + x, PAIRS, stride=16), :] for k in range(4)], 0)
                )
            r = left(y_in[pl.ds(0, 192)], y_in[pl.ds(192, 192)], jnp.concatenate(cols, 1))
            for i in range(2):
                x = 2 * pair + i
                tiles = packed([r[48 * j : 48 * j + 48, 128 * i : 128 * i + 128] for j in range(4)])
                for t in range(3):
                    for c in range(2):
                        wire[pl.ds(b * BAND + t * 24 + c * OWN + x, 24, stride=72), :] = tiles[t][24 * c : 24 * c + 24]
            return carry

        lax.fori_loop(0, OWN // 2, ky, 0)

        @pl.when(b == 0)
        def _():
            pl.semaphore_wait(barrier, SLABS - 1 + GROUPS - 1)

        for d, q in slab_peers:
            send_line(b, d, q).start()
        own_line(b).start()
        return carry

    def send_line(b, d, q):
        return slab_copy(
            wire.at[pl.ds(b * BAND + q * BLOCK, BLOCK)],
            lines.at[pl.ds(b * BAND + me * BLOCK, BLOCK)],
            w_s.at[b, d],
            w_r.at[b, d],
            q,
        )

    def own_line(b):
        at = pl.ds(b * BAND + me * BLOCK, BLOCK)
        return pltpu.make_async_copy(wire.at[at], lines.at[at], own_sem.at[b])

    lax.fori_loop(0, BANDS, first, 0)

    def send_pot(d, q):
        return slab_copy(
            pot.at[:, pl.ds(pl.multiple_of(q * LINE, 128), LINE)], vb.at[me], pot_s.at[d], pot_r.at[d], q
        )

    for d, q in slab_peers:
        send_pot(d, q).start()
    own_pot = pltpu.make_async_copy(
        pot.at[:, pl.ds(pl.multiple_of(me * LINE, 128), LINE)], vb.at[me], own_sem.at[BANDS]
    )
    own_pot.start()

    for i in range(8):
        ksq = ky2[...] + kxz[grp, i : i + 1, :]
        zero = ksq == 0.0
        green[:, 128 * i : 128 * i + 128] = jnp.where(zero, 0.0, 4.0 * math.pi / jnp.where(zero, 1.0, ksq))

    dens[...] = jnp.zeros_like(dens)

    def lines_x(b, carry):
        own_line(b).wait()
        for d, q in slab_peers:
            send_line(b, d, q).wait_recv()

        def kx(a, carry):
            x = jnp.concatenate(
                [
                    jnp.concatenate(
                        [lines[pl.ds(b * BAND + s * BLOCK + (3 * a + t) * 24, 24)] for s in range(SLABS)], 0
                    )
                    for t in range(3)
                ],
                1,
            )
            r = left(x_in[pl.ds(0, 192)], x_in[pl.ds(192, 192)], x)
            at = pl.ds(pl.multiple_of(a * 384, 128), 384)
            moved[b, :, at] = r
            dens[:, at] += r[:GRID] * r[:GRID] + r[GRID:] * r[GRID:]
            return carry

        lax.fori_loop(0, 3, kx, 0)
        return carry

    lax.fori_loop(0, BANDS, lines_x, 0)

    dq[...] = left(qx[pl.ds(0, 128)], qx[pl.ds(128, 128)], dens[...])

    def send_part(d, q):
        return band_copy(dq.at[pl.ds(pl.multiple_of(q * 8, 8), 8)], part.at[grp], rs_s.at[d], rs_r.at[d], q)

    for d, q in band_peers:
        send_part(d, q).start()
    total = dq[pl.ds(pl.multiple_of(grp * 8, 8), 8)]
    own_pot.wait()
    for d, q in slab_peers:
        send_pot(d, q).wait_recv()
    for s in range(SLABS):
        vl[OWN * s : OWN * s + OWN, :] = vb[s]
    for d, q in band_peers:
        send_part(d, q).wait_recv()
    for d, q in band_peers:
        total = total + part[q]
    share[...] = total

    def send_share(d, q):
        return slab_copy(share, whole.at[me], ag_s.at[d], ag_r.at[d], q)

    for d, q in slab_peers:
        send_share(d, q).start()
    whole[me] = total
    for d, q in slab_peers:
        send_share(d, q).wait_recv()
    for a in range(3):
        tiles = [
            jnp.concatenate([whole[s, :, 384 * a + 128 * t : 384 * a + 128 * t + 128] for s in range(SLABS)], 0)
            for t in range(3)
        ]
        x = jnp.concatenate(unpacked(tiles), 0)
        zt[pl.ds(256 * a, 256)] = times(x, qz[pl.ds(0, 128)], qz[pl.ds(128, 128)])
    x = jnp.concatenate([zt[pl.ds(i, GRID, stride=8), :] for i in range(8)], 1)
    x = left(qy[pl.ds(0, GRID)], qy[pl.ds(GRID, GRID)], x) * green[...]
    x = left(qyt[me, 0:16], qyt[me, 16:32], x)
    x = jnp.concatenate([x[:, 128 * i : 128 * i + 128] for i in range(8)], 0)
    zt[pl.ds(0, 128)] = times(x, qzt[pl.ds(0, 128)], qzt[pl.ds(128, 128)])
    for a in range(3):
        tiles = packed([zt[pl.ds(4 * a + j, 8, stride=16), :] for j in range(4)])
        for t in range(3):
            modes[:, 384 * a + 128 * t : 384 * a + 128 * t + 128] = tiles[t]

    def send_modes(d, q):
        return band_copy(modes, hq.at[pl.ds(pl.multiple_of(grp * 8, 8), 8)], hq_s.at[d], hq_r.at[d], q)

    for d, q in band_peers:
        send_modes(d, q).start()
    hq[pl.ds(pl.multiple_of(grp * 8, 8), 8)] = modes[...]
    for d, q in band_peers:
        send_modes(d, q).wait_recv()
    h = left(qxt[pl.ds(0, GRID)], qxt[pl.ds(GRID, GRID)], hq[...])
    hart[...] = h
    s, c = sin_cos((vl[...] + h) * TIME_STEP)
    sinb[...] = s
    cosb[...] = c

    def send_back(b, d, q):
        return slab_copy(
            back.at[pl.ds(b * BAND + q * BLOCK, BLOCK)],
            home.at[pl.ds(b * BAND + me * BLOCK, BLOCK)],
            b_s.at[b, d],
            b_r.at[b, d],
            q,
        )

    def own_back(b):
        at = pl.ds(b * BAND + me * BLOCK, BLOCK)
        return pltpu.make_async_copy(back.at[at], home.at[at], own_sem.at[b])

    def kick(b, carry):
        def kx(a, carry):
            at = pl.ds(pl.multiple_of(a * 384, 128), 384)
            re = moved[b, 0:GRID, at]
            im = moved[b, GRID : 2 * GRID, at]
            cs = cosb[:, at]
            sn = sinb[:, at]
            x = jnp.concatenate([re * cs + im * sn, im * cs - re * sn], 0)
            r = left(x_out[pl.ds(0, 192)], x_out[pl.ds(192, 192)], x)
            for q in range(SLABS):
                for t in range(3):
                    back[pl.ds(b * BAND + q * BLOCK + (3 * a + t) * 24, 24)] = r[24 * q : 24 * q + 24, 128 * t : 128 * t + 128]
            return carry

        lax.fori_loop(0, 3, kx, 0)
        for d, q in slab_peers:
            send_back(b, d, q).start()
        own_back(b).start()
        return carry

    lax.fori_loop(0, BANDS, kick, 0)

    for q in range(SLABS):
        hs[q] = hart[OWN * q : OWN * q + OWN, :]

    def send_hart(d, q):
        return slab_copy(
            hs.at[q], har.at[:, pl.ds(pl.multiple_of(me * LINE, 128), LINE)], h_s.at[d], h_r.at[d], q
        )

    for d, q in slab_peers:
        send_hart(d, q).start()
    own_hart = pltpu.make_async_copy(
        hs.at[me], har.at[:, pl.ds(pl.multiple_of(me * LINE, 128), LINE)], own_sem.at[BANDS]
    )
    own_hart.start()

    def store(b):
        return pltpu.make_async_copy(ob.at[b], ev.at[b], out_sem.at[b])

    def last(b, carry):
        own_back(b).wait()
        for d, q in slab_peers:
            send_back(b, d, q).wait_recv()

        def ky(pair, carry):
            cols = []
            for i in range(2):
                x = 2 * pair + i
                tiles = [
                    jnp.concatenate(
                        [home[pl.ds(b * BAND + t * 24 + c * OWN + x, 24, stride=72), :] for c in range(2)], 0
                    )
                    for t in range(3)
                ]
                cols.append(jnp.concatenate(unpacked(tiles), 0))
            r = left(y_out[pl.ds(0, 192)], y_out[pl.ds(192, 192)], jnp.concatenate(cols, 1))
            for i in range(2):
                x = 2 * pair + i
                for k in range(4):
                    plane[pl.ds(768 * k + x, PAIRS, stride=16), :] = r[48 * k : 48 * k + 48, 128 * i : 128 * i + 128]
            return carry

        lax.fori_loop(0, OWN // 2, ky, 0)

        def kz(chunk, carry):
            res = []
            for j in range(2):
                x = jnp.concatenate(
                    [plane[pl.ds(pl.multiple_of(768 * (2 * j + c) + chunk * 128, 128), 128)] for c in range(2)], 1
                )
                res.append(times(x, z_out[pl.ds(512 * j, 256)], z_out[pl.ds(512 * j + 256, 256)]))
            tiles = (res[0][:, :128], res[0][:, 128:] + res[1][:, :128], res[1][:, 128:])
            start = pl.multiple_of(chunk * (8 * 384), 128)
            for i in range(8):
                for t in range(3):
                    ob[b, :, pl.ds(start + 384 * i + 128 * t, 128)] = tiles[t][16 * i : 16 * i + OWN]
            return carry

        lax.fori_loop(0, 6, kz, 0)
        store(b).start()
        return carry

    lax.fori_loop(0, BANDS, last, 0)

    own_hart.wait()
    for d, q in slab_peers:
        send_hart(d, q).wait()
        send_pot(d, q).wait_send()
        send_share(d, q).wait_send()
    for d, q in band_peers:
        send_part(d, q).wait_send()
        send_modes(d, q).wait_send()

    def drain(b, carry):
        for d, q in slab_peers:
            send_line(b, d, q).wait_send()
            send_back(b, d, q).wait_send()
        store(b).wait()
        return carry

    lax.fori_loop(0, BANDS, drain, 0)


def body(orbitals, potential):
    t = tables()
    consts = [jnp.asarray(t[name]) for name in NAMES]
    vmem = lambda *shape: pltpu.VMEM(shape, F32)
    dma = lambda *shape: pltpu.SemaphoreType.DMA(shape)
    ev, har = pl.pallas_call(
        kernel,
        out_shape=(
            jax.ShapeDtypeStruct(orbitals.shape, F32),
            jax.ShapeDtypeStruct(potential.shape, F32),
        ),
        in_specs=[pl.BlockSpec(memory_space=pl.ANY)] * 2 + [pl.BlockSpec(memory_space=pltpu.VMEM)] * len(consts),
        out_specs=[pl.BlockSpec(memory_space=pl.ANY)] * 2,
        scratch_shapes=[
            vmem(BANDS, OWN, 2 * GRID * GRID),
            vmem(4 * 768, 128),
            vmem(BANDS * BAND, 128),
            vmem(BANDS * BAND, 128),
            vmem(BANDS, 2 * GRID, LINE),
            vmem(BANDS * BAND, 128),
            vmem(BANDS * BAND, 128),
            vmem(BANDS, OWN, 2 * GRID * GRID),
            vmem(GRID, LINE),
            vmem(128, LINE),
            vmem(GROUPS, 8, LINE),
            vmem(8, LINE),
            vmem(8, LINE),
            vmem(SLABS, 8, LINE),
            vmem(768, 128),
            vmem(GRID, 1024),
            vmem(128, LINE),
            vmem(GRID, LINE),
            vmem(SLABS, OWN, LINE),
            vmem(GRID, LINE),
            vmem(GRID, LINE),
            vmem(GRID, LINE),
            vmem(SLABS, OWN, LINE),
            dma(BANDS), dma(BANDS),
            dma(SLABS), dma(SLABS),
            dma(BANDS, SLABS), dma(BANDS, SLABS),
            dma(BANDS, SLABS), dma(BANDS, SLABS),
            dma(GROUPS), dma(GROUPS),
            dma(SLABS), dma(SLABS),
            dma(GROUPS), dma(GROUPS),
            dma(SLABS), dma(SLABS),
            dma(BANDS + 1),
        ],
        compiler_params=pltpu.CompilerParams(
            collective_id=0, has_side_effects=True, vmem_limit_bytes=56 * 1024 * 1024
        ),
    )(orbitals, potential, *consts)
    return ev, har


def solution(mesh):
    return jax.shard_map(
        body,
        mesh=mesh,
        in_specs=(P("band", "slab", None), P("slab", None)),
        out_specs=(P("band", "slab", None), P("slab", None)),
        check_vma=False,
    )
```

profile of v0, /device:TPU:1, one launch (start us, length us, event | category | flops | bytes accessed | tf_op | source)
XLA Modules:
  0.0 143.0 jit_solution(10320458302099059392)
XLA Ops:
  0.6 6.2 %copy.18.orb = f32[4,12,18432]{2,1,0:T(8,128)} copy(f32[4,12,18432]{2,0,1:T(4,128)} %param.16) | data formatting | bytes 7077888 | tf_op args[0]
  6.8 128.9 %shard_map.167 = (f32[4,12,18432]{2,1,0:T(8,128)}, f32[12,9216]{1,0:T(8,128)}) custom-call(f32[4,12,18432]{2,1,0:T(8,128)} %copy.18.orb, f32[12,9216]{1,0:T(8,128)} %pot.1, bf16[1024,256]{1,0:T(8,128)(2,1)} %constant.28.clone.z_in, bf16[1024,256]{1,0:T(8,128)(2,1)} %constant.29.clone.z_out, bf16[384,192]{1,0:T(8,128)(2,1)} %constant.30.clone.y_in, ...), custom_call_target="tpu_custom_call" | custom-call | tf_op jit(solution)/shard_map/pallas_call | solution.py:495
  135.7 0.0 copy-start
  135.7 6.5 %copy.19 = f32[4,12,18432]{2,0,1:T(4,128)} copy(f32[4,12,18432]{2,1,0:T(8,128)} %get-tuple-element.2) | data formatting | bytes 7077888 | tf_op jit(solution)/shard_map/pallas_call | solution.py:495
  142.2 0.0 copy-done
  142.2 0.8 copy.21
Async XLA Ops:
  135.7 6.5 %copy-start = (f32[12,9216]{1,0:T(8,128)S(1)}, f32[12,9216]{1,0:T(8,128)}, u32[]{:S(2)}) copy-start(f32[12,9216]{1,0:T(8,128)} %get-tuple-element.7) | copy-start | bytes 1327108
where the time goes:
time: 143 us
  Pallas kernels  129 us (90%)
  local copies, waits for them, and re-layouts  13.4 us (9%)
    pallas_call x1, Pallas kernels, body(): pl.pallas_call(kernel, out_shape=(jax.ShapeDtypeStruct(orbitals.shape, F3...  129 us
    unnamed x4, local copies, waits for them, and re-layouts  6.98 us
    pallas_call x1, local copies, waits for them, and re-layouts, body(): pl.pallas_call(kernel, out_shape=(jax.ShapeDtypeStruct(orbitals.shape, F3...  6.47 us

commit v1 on v0

v1 whole, which is shorter than its diff:
```python
import functools
import math

import jax
import jax.numpy as jnp
import ml_dtypes
import numpy as np
from jax import lax
from jax.experimental import pallas as pl
from jax.experimental.pallas import tpu as pltpu
from jax.sharding import PartitionSpec as P

GRID = 96
TIME_STEP = 0.1
MESH = pl.DeviceIdType.MESH
SLABS = 8
GROUPS = 16
BANDS = 4
OWN = GRID // SLABS
LINE = OWN * GRID
TILES = LINE // 128
BLOCK = TILES * 2 * OWN
BAND = SLABS * BLOCK
XROWS = 2 * GRID * GRID // 128 * BANDS
PAIRS = GRID // 2
SHARE = GRID // GROUPS
SCALE = 1.88474
F32 = jnp.float32
BF16 = jnp.bfloat16


def half_step_line():
    n = np.arange(GRID)
    m = (n + GRID // 2) % GRID - GRID // 2
    k = 2.0 * math.pi / GRID * m
    phase = np.exp(-1j * k * k * TIME_STEP / 4)
    exact = np.fft.ifft(phase) / SCALE
    line = np.stack([exact.real, exact.imag]).astype(np.float32).astype(ml_dtypes.bfloat16).astype(np.float64)

    def worst(values):
        return np.abs(np.fft.fft((values[0] + 1j * values[1]) * SCALE) - phase).max()

    now = worst(line)
    for _ in range(3):
        for part in range(2):
            for t in range(GRID // 2 + 1):
                for sign in (1.0, -1.0):
                    trial = line.copy()
                    step = 2.0 ** (math.floor(math.log2(abs(line[part, t]))) - 7)
                    trial[part, [t, -t % GRID]] = line[part, t] + sign * step
                    error = worst(trial)
                    if error < 0.9999 * now:
                        now, line = error, trial
    return line


def half_step_factor():
    n = np.arange(GRID)
    real, imag = half_step_line()[:, (n[:, None] - n[None, :]) % GRID]
    out = np.zeros((2, GRID, 2, GRID))
    out[0, :, 0] = real
    out[0, :, 1] = -imag
    out[1, :, 0] = imag
    out[1, :, 1] = real
    return out


def real_basis():
    n = np.arange(GRID)
    rows, ksq = [np.full(GRID, 1.0 / math.sqrt(GRID))], [0.0]
    for m in range(1, GRID // 2):
        angle = 2.0 * math.pi * ((m * n) % GRID) / GRID
        rows += [np.cos(angle) * math.sqrt(2.0 / GRID), np.sin(angle) * math.sqrt(2.0 / GRID)]
        ksq += [(2.0 * math.pi * m / GRID) ** 2] * 2
    rows.append(np.where(n % 2 == 0, 1.0, -1.0) / math.sqrt(GRID))
    ksq.append(math.pi**2)
    return np.stack(rows), np.array(ksq)


def exact(matrix):
    return matrix.astype(ml_dtypes.bfloat16)


def split(matrix):
    high = matrix.astype(np.float32).astype(ml_dtypes.bfloat16)
    low = (matrix - high.astype(np.float64)).astype(ml_dtypes.bfloat16)
    return np.stack([high, low])


@functools.lru_cache(maxsize=None)
def tables():
    g = half_step_factor()
    t = {}
    into = g.transpose(2, 3, 0, 1)
    padded = np.zeros((2, GRID, 2, 128))
    padded[..., :GRID] = into
    padded = padded.reshape(2 * GRID, 256)
    za = np.zeros((2, 256, 256))
    za[0, :192] = padded
    za[1, 64:] = padded
    t["z_in"] = exact(za.reshape(512, 256))
    rows = np.zeros((2, 128, 2, GRID))
    rows[:, :GRID] = into
    rows = rows.reshape(256, 2 * GRID)
    zb = np.zeros((2, 256, 256))
    zb[0, :, :192] = rows
    zb[1, :, 64:] = rows
    t["z_out"] = exact(zb.reshape(512, 256))
    j, s, a = np.meshgrid(np.arange(4), np.arange(SLABS), np.arange(3), indexing="ij")
    wire_y = 12 * s + 4 * a + j
    pair_y = 2 * np.arange(PAIRS)[None, :] + np.arange(2)[:, None]
    ky = g[:, wire_y][:, :, :, :, :, pair_y]
    t["y_in"] = exact(ky.transpose(1, 0, 2, 3, 5, 4, 6).reshape(192, 192))
    ky = g[:, pair_y][:, :, :, :, wire_y]
    t["y_out"] = exact(ky.transpose(1, 0, 2, 4, 3, 5, 6).reshape(192, 192))
    kx = g.reshape(2, GRID, 2, SLABS, OWN)
    t["x_in"] = exact(kx.transpose(0, 1, 3, 2, 4).reshape(192, 192))
    kx = g.reshape(2, SLABS, OWN, 2, GRID)
    t["x_out"] = exact(kx.transpose(1, 0, 2, 3, 4).reshape(192, 192))
    q, ksq = real_basis()
    qx = np.zeros((GROUPS, 8, GRID))
    qx[:, :SHARE] = q.reshape(GROUPS, SHARE, GRID)
    qx = qx.reshape(128, GRID)
    t["qx"] = split(qx * SCALE**6).reshape(256, GRID)
    t["qxt"] = split(qx.T).reshape(192, 128)
    qz = np.zeros((128, 128))
    qz[:GRID, :GRID] = q.T
    t["qz"] = split(qz).reshape(256, 128)
    t["qzt"] = split(qz.T).reshape(256, 128)
    aj_s = 12 * np.arange(SLABS)[None, :] + np.arange(OWN)[:, None]
    t["qy"] = split(q[:, aj_s.reshape(-1)]).reshape(192, GRID)
    qyt = np.zeros((SLABS, 16, GRID))
    qyt[:, :OWN] = q.T.reshape(SLABS, OWN, GRID)
    t["qyt"] = split(qyt).transpose(1, 0, 2, 3).reshape(SLABS, 32, GRID)
    kxz = np.ones((GROUPS, 8, 128))
    kxz[:, :SHARE, :GRID] = ksq.reshape(GROUPS, SHARE)[:, :, None] + ksq[None, None, :]
    t["kxz"] = kxz.astype(np.float32)
    t["ky2"] = np.broadcast_to(ksq[:, None], (GRID, 128)).astype(np.float32)
    return t


NAMES = ("z_in", "y_in", "x_in", "kxz", "ky2", "qx", "qz", "qy", "qyt", "qzt", "qxt", "x_out", "y_out", "z_out")


def halves(x):
    high = x.astype(BF16)
    return high, (x - high.astype(F32)).astype(BF16)


def dot(a, b):
    return jnp.dot(a, b, preferred_element_type=F32)


def times(x, high, low):
    xh, xl = halves(x)
    return dot(xh, high) + (dot(xl, high) + dot(xh, low))


def left(high, low, x):
    xh, xl = halves(x)
    return dot(high, xh) + (dot(high, xl) + dot(low, xh))


def sin_cos(t):
    n = jnp.round(t * (2.0 / math.pi))
    r = t - n * 1.5703125
    r = r - n * 4.8375129699707031e-4
    r = r - n * 7.5495649e-08
    r2 = r * r
    sine = r + r * r2 * (-1.6666654611e-1 + r2 * (8.3321608736e-3 + r2 * -1.9515295891e-4))
    cosine = 1.0 - 0.5 * r2 + r2 * r2 * (4.166664568298827e-2 + r2 * (-1.388731625493765e-3 + r2 * 2.443315711809948e-5))
    quarter = n.astype(jnp.int32) & 3
    odd = (quarter & 1) == 1
    s = jnp.where(odd, cosine, sine)
    c = jnp.where(odd, sine, cosine)
    s = jnp.where(quarter >= 2, -s, s)
    c = jnp.where((quarter == 1) | (quarter == 2), -c, c)
    return s, c


def times2(x, table):
    r = dot(jnp.concatenate(halves(x), 0), table)
    return r[: x.shape[0]] + r[x.shape[0] :]


def left2(table, x):
    r = dot(table, jnp.concatenate(halves(x), 1))
    return r[:, : x.shape[1]] + r[:, x.shape[1] :]


def lane_of(shape):
    return lax.broadcasted_iota(jnp.int32, shape, len(shape) - 1)


def packed(parts):
    lane = lane_of(parts[0].shape)
    r1 = pltpu.roll(parts[1], 96, 1)
    r2 = pltpu.roll(parts[2], 64, 1)
    r3 = pltpu.roll(parts[3], 32, 1)
    return (
        jnp.where(lane < 96, parts[0], r1),
        jnp.where(lane < 64, r1, r2),
        jnp.where(lane < 32, r2, r3),
    )


def unpacked(tiles):
    lane = lane_of(tiles[0].shape)
    return (
        tiles[0],
        pltpu.roll(jnp.where(lane < 64, tiles[1], tiles[0]), 32, 1),
        pltpu.roll(jnp.where(lane < 32, tiles[2], tiles[1]), 64, 1),
        pltpu.roll(tiles[2], 96, 1),
    )


def kernel(orb, pot, *refs):
    sources, refs = refs[: len(NAMES)], refs[len(NAMES) :]
    ev, har, refs = refs[0], refs[1], refs[2:]
    consts, refs = refs[: len(NAMES)], refs[len(NAMES) :]
    z_in, y_in, x_in, kxz, ky2, qx, qz, qy, qyt, qzt, qxt, x_out, y_out, z_out = consts
    (
     ib, wire, lines, moved, back, home, ob, dens, dq, part, share, modes, whole, zt, green, hq, hart,
           vb, vl, cosb, sinb, hs, hrow, harv,
           in_sem, out_sem, pot_s, pot_r, w_s, w_r, b_s, b_r, rs_s, rs_r, ag_s, ag_r, hq_s, hq_r, h_s, h_r, g_s, g_r, own_sem, const_sem, tail_s, tail_r, head_s, head_r) = refs
    me = lax.axis_index("slab")
    grp = lax.axis_index("band")
    slab_peers = [(d, lax.rem(me + d, SLABS)) for d in range(1, SLABS)]
    band_peers = [(d, lax.rem(grp + d, GROUPS)) for d in range(1, GROUPS)]

    barrier = pltpu.get_barrier_semaphore()
    for _, q in slab_peers:
        pl.semaphore_signal(barrier, inc=1, device_id={"slab": q}, device_id_type=MESH)
    for _, q in band_peers:
        pl.semaphore_signal(barrier, inc=1, device_id={"band": q}, device_id_type=MESH)

    def load(i):
        at = pl.ds(i * XROWS, XROWS)
        return pltpu.make_async_copy(orb.at[at], ib.at[at], in_sem.at[i])

    def table(i):
        return pltpu.make_async_copy(sources[i], consts[i], const_sem.at[i])

    table(0).start()
    table(1).start()
    for i in range(OWN):
        load(i).start()
    for i in range(2, len(NAMES)):
        table(i).start()
    table(0).wait()
    table(1).wait()

    def slab_copy(src, dst, s, r, q):
        return pltpu.make_async_remote_copy(src, dst, s, r, device_id={"slab": q}, device_id_type=MESH)

    def band_copy(src, dst, s, r, q):
        return pltpu.make_async_remote_copy(src, dst, s, r, device_id={"band": q}, device_id_type=MESH)

    def first(b, carry):
        def local(pair, carry):
            @pl.when(b == 0)
            def _():
                for i in range(2):
                    load(2 * pair + i).wait()

            tiles = [
                jnp.concatenate(
                    [ib[pl.ds((2 * pair + i) * XROWS + 4 * t + b, PAIRS, stride=12), :] for i in range(2)], 0
                )
                for t in range(3)
            ]
            z = []
            for j in range(2):
                x = jnp.concatenate([tiles[j], tiles[j + 1]], 1)
                z.append(times2(x, z_in[pl.ds(256 * j, 256)]))
            x = jnp.concatenate(
                [
                    jnp.concatenate(
                        [z[j][48 * i : 48 * i + 48, 128 * c : 128 * c + 128] for j in range(2) for c in range(2)], 0
                    )
                    for i in range(2)
                ],
                1,
            )
            r = left2(y_in[...], x)
            for i in range(2):
                x = 2 * pair + i
                tiles = packed([r[48 * j : 48 * j + 48, 128 * i : 128 * i + 128] for j in range(4)])
                for t in range(3):
                    for c in range(2):
                        wire[pl.ds(b * BAND + t * 24 + c * OWN + x, 24, stride=72), :] = tiles[t][24 * c : 24 * c + 24]
            return carry

        lax.fori_loop(0, OWN // 2, local, 0)

        @pl.when(b == 0)
        def _():
            pl.semaphore_wait(barrier, SLABS - 1 + GROUPS - 1)

        @pl.when(b < BANDS - 1)
        def _():
            for d, q in slab_peers:
                send_line(b, d, q).start()

        @pl.when(b == BANDS - 1)
        def _():
            for a in range(3):
                for d, q in slab_peers:
                    send_tail(a, d, q).start()

        own_line(b).start()
        return carry

    def send_tail(a, d, q):
        return slab_copy(
            wire.at[pl.ds((BANDS - 1) * BAND + q * BLOCK + 72 * a, 72)],
            lines.at[pl.ds((BANDS - 1) * BAND + me * BLOCK + 72 * a, 72)],
            tail_s.at[a, d],
            tail_r.at[a, d],
            q,
        )

    def send_line(b, d, q):
        return slab_copy(
            wire.at[pl.ds(b * BAND + q * BLOCK, BLOCK)],
            lines.at[pl.ds(b * BAND + me * BLOCK, BLOCK)],
            w_s.at[b, d],
            w_r.at[b, d],
            q,
        )

    def own_line(b):
        at = pl.ds(b * BAND + me * BLOCK, BLOCK)
        return pltpu.make_async_copy(wire.at[at], lines.at[at], own_sem.at[b])

    lax.fori_loop(0, BANDS, first, 0)

    def send_pot(d, q):
        return slab_copy(
            pot.at[:, pl.ds(pl.multiple_of(q * LINE, 128), LINE)], vb.at[me], pot_s.at[d], pot_r.at[d], q
        )

    for d, q in slab_peers:
        send_pot(d, q).start()
    own_pot = pltpu.make_async_copy(
        pot.at[:, pl.ds(pl.multiple_of(me * LINE, 128), LINE)], vb.at[me], own_sem.at[BANDS]
    )
    own_pot.start()

    for i in range(2, len(NAMES)):
        table(i).wait()

    for i in range(8):
        ksq = ky2[...] + kxz[grp, i : i + 1, :]
        zero = ksq == 0.0
        green[:, 128 * i : 128 * i + 128] = jnp.where(zero, 0.0, 4.0 * math.pi / jnp.where(zero, 1.0, ksq))

    dens[...] = jnp.zeros_like(dens)

    def kx_in(b, a):
        x = jnp.concatenate(
            [
                jnp.concatenate(
                    [lines[pl.ds(b * BAND + s * BLOCK + (3 * a + t) * 24, 24)] for s in range(SLABS)], 0
                )
                for t in range(3)
            ],
            1,
        )
        r = left2(x_in[...], x)
        at = pl.ds(pl.multiple_of(a * 384, 128), 384)
        moved[b, :, at] = r
        dens[:, at] += r[:GRID] * r[:GRID] + r[GRID:] * r[GRID:]

    def lines_x(b, carry):
        own_line(b).wait()
        for d, q in slab_peers:
            send_line(b, d, q).wait_recv()

        def chunk(a, carry):
            kx_in(b, a)
            return carry

        lax.fori_loop(0, 3, chunk, 0)
        return carry

    lax.fori_loop(0, BANDS - 1, lines_x, 0)

    def send_part(a, d, q):
        at = pl.ds(pl.multiple_of(a * 384, 128), 384)
        return band_copy(dq.at[pl.ds(pl.multiple_of(q * 8, 8), 8), at], part.at[grp, :, at], rs_s.at[a, d], rs_r.at[a, d], q)

    own_line(BANDS - 1).wait()

    def last_lines(a, carry):
        for d, q in slab_peers:
            send_tail(a, d, q).wait_recv()
        kx_in(BANDS - 1, a)
        at = pl.ds(pl.multiple_of(a * 384, 128), 384)
        dq[:, at] = left(qx[pl.ds(0, 128)], qx[pl.ds(128, 128)], dens[:, at])
        for d, q in band_peers:
            send_part(a, d, q).start()
        return carry

    lax.fori_loop(0, 3, last_lines, 0)

    own_pot.wait()
    for d, q in slab_peers:
        send_pot(d, q).wait_recv()
    for s in range(SLABS):
        vl[OWN * s : OWN * s + OWN, :] = vb[s]

    def send_share(a, d, q):
        at = pl.ds(pl.multiple_of(a * 384, 128), 384)
        return slab_copy(share.at[:, at], whole.at[me, :, at], ag_s.at[a, d], ag_r.at[a, d], q)

    def sums(a, carry):
        at = pl.ds(pl.multiple_of(a * 384, 128), 384)
        for d, q in band_peers:
            send_part(a, d, q).wait_recv()
        total = dq[pl.ds(pl.multiple_of(grp * 8, 8), 8), at]
        for d, q in band_peers:
            total = total + part[q, :, at]
        share[:, at] = total
        for d, q in slab_peers:
            send_share(a, d, q).start()
        whole[me, :, at] = total
        return carry

    lax.fori_loop(0, 3, sums, 0)

    def along_z(a, carry):
        for d, q in slab_peers:
            send_share(a, d, q).wait_recv()
        tiles = [
            jnp.concatenate(
                [whole[s, :, pl.ds(pl.multiple_of(384 * a + 128 * t, 128), 128)] for s in range(SLABS)], 0
            )
            for t in range(3)
        ]
        x = jnp.concatenate(unpacked(tiles), 0)
        zt[pl.ds(pl.multiple_of(256 * a, 256), 256)] = times(x, qz[pl.ds(0, 128)], qz[pl.ds(128, 128)])
        return carry

    lax.fori_loop(0, 3, along_z, 0)
    x = jnp.concatenate([zt[pl.ds(i, GRID, stride=8), :] for i in range(8)], 1)
    x = left(qy[pl.ds(0, GRID)], qy[pl.ds(GRID, GRID)], x) * green[...]
    x = left(qyt[me, 0:16], qyt[me, 16:32], x)
    x = jnp.concatenate([x[:, 128 * i : 128 * i + 128] for i in range(8)], 0)
    zt[pl.ds(0, 128)] = times(x, qzt[pl.ds(0, 128)], qzt[pl.ds(128, 128)])
    for a in range(3):
        tiles = packed([zt[pl.ds(4 * a + j, 8, stride=16), :] for j in range(4)])
        for t in range(3):
            modes[:, 384 * a + 128 * t : 384 * a + 128 * t + 128] = tiles[t]

    def send_modes(d, q):
        return band_copy(modes, hq.at[pl.ds(pl.multiple_of(grp * 8, 8), 8)], hq_s.at[d], hq_r.at[d], q)

    for d, q in band_peers:
        send_modes(d, q).start()
    hq[pl.ds(pl.multiple_of(grp * 8, 8), 8)] = modes[...]
    for d, q in band_peers:
        send_modes(d, q).wait_recv()
    def send_back(b, d, q):
        return slab_copy(
            back.at[pl.ds(b * BAND + q * BLOCK, BLOCK)],
            home.at[pl.ds(b * BAND + me * BLOCK, BLOCK)],
            b_s.at[b, d],
            b_r.at[b, d],
            q,
        )

    def own_back(b):
        at = pl.ds(b * BAND + me * BLOCK, BLOCK)
        return pltpu.make_async_copy(back.at[at], home.at[at], own_sem.at[b])

    def send_head(a, d, q):
        return slab_copy(
            back.at[pl.ds(q * BLOCK + 72 * a, 72)],
            home.at[pl.ds(me * BLOCK + 72 * a, 72)],
            head_s.at[a, d],
            head_r.at[a, d],
            q,
        )

    def kx_out(b, a):
        at = pl.ds(pl.multiple_of(a * 384, 128), 384)
        re = moved[b, 0:GRID, at]
        im = moved[b, GRID : 2 * GRID, at]
        cs = cosb[:, at]
        sn = sinb[:, at]
        x = jnp.concatenate([re * cs + im * sn, im * cs - re * sn], 0)
        r = left2(x_out[...], x)
        for q in range(SLABS):
            for t in range(3):
                back[pl.ds(b * BAND + q * BLOCK + (3 * a + t) * 24, 24)] = r[24 * q : 24 * q + 24, 128 * t : 128 * t + 128]

    def head(a, carry):
        at = pl.ds(pl.multiple_of(a * 384, 128), 384)
        h = left(qxt[pl.ds(0, GRID)], qxt[pl.ds(GRID, GRID)], hq[:, at])
        hart[:, at] = h
        s, c = sin_cos((vl[:, at] + h) * TIME_STEP)
        sinb[:, at] = s * SCALE**6
        cosb[:, at] = c * SCALE**6
        kx_out(0, a)
        for d, q in slab_peers:
            send_head(a, d, q).start()
        return carry

    lax.fori_loop(0, 3, head, 0)
    own_back(0).start()

    for t in range(TILES):
        hs[pl.ds(t, GRID, stride=16), :] = hart[:, 128 * t : 128 * t + 128]

    def send_row(d, q):
        return slab_copy(
            hs.at[pl.ds((q * OWN + grp) * 16, 16)],
            hrow.at[pl.ds((grp * SLABS + me) * 16, 16)],
            h_s.at[d],
            h_r.at[d],
            q,
        )

    own_row = pltpu.make_async_copy(
        hs.at[pl.ds((me * OWN + grp) * 16, 16)], hrow.at[pl.ds((grp * SLABS + me) * 16, 16)], own_sem.at[BANDS]
    )

    def send_rows(d, q, g):
        at = pl.ds(g * (SLABS * 16), SLABS * 16)
        return band_copy(hrow.at[at], hrow.at[at], g_s.at[d], g_r.at[d], q)

    @pl.when(grp < OWN)
    def _():
        own_row.start()
        for d, q in slab_peers:
            send_row(d, q).start()

    def kick(b, carry):
        def chunk(a, carry):
            kx_out(b, a)
            return carry

        lax.fori_loop(0, 3, chunk, 0)
        for d, q in slab_peers:
            send_back(b, d, q).start()
        own_back(b).start()
        return carry

    lax.fori_loop(1, BANDS, kick, 0)

    def store(i):
        at = pl.ds(i * XROWS, XROWS)
        return pltpu.make_async_copy(ob.at[at], ev.at[at], out_sem.at[i])

    def rows_out():
        @pl.when(grp < OWN)
        def _():
            own_row.wait()
            for d, q in slab_peers:
                send_row(d, q).wait_recv()
            for d, q in band_peers:
                send_rows(d, q, grp).start()

    def rows_in():
        for d, _ in band_peers:
            source = lax.rem(grp + GROUPS - d, GROUPS)

            @pl.when(source < OWN)
            def _():
                send_rows(d, source, source).wait_recv()

        for s in range(SLABS):
            for t in range(TILES):
                harv[:, LINE * s + 128 * t : LINE * s + 128 * t + 128] = hrow[
                    pl.ds(16 * s + t, OWN, stride=SLABS * 16), :
                ]
        out_hart.start()

    out_hart = pltpu.make_async_copy(harv, har, own_sem.at[BANDS])

    def last(b, carry):
        @pl.when(b == 1)
        def _():
            rows_out()

        @pl.when(b == 3)
        def _():
            rows_in()

        own_back(b).wait()

        @pl.when(b == 0)
        def _():
            for a in range(3):
                for d, q in slab_peers:
                    send_head(a, d, q).wait_recv()

        @pl.when(b > 0)
        def _():
            for d, q in slab_peers:
                send_back(b, d, q).wait_recv()

        def local(pair, carry):
            cols = []
            for i in range(2):
                x = 2 * pair + i
                tiles = [
                    jnp.concatenate(
                        [home[pl.ds(b * BAND + t * 24 + c * OWN + x, 24, stride=72), :] for c in range(2)], 0
                    )
                    for t in range(3)
                ]
                cols.append(jnp.concatenate(unpacked(tiles), 0))
            r = left2(y_out[...], jnp.concatenate(cols, 1))
            res = []
            for j in range(2):
                x = jnp.concatenate(
                    [
                        jnp.concatenate(
                            [r[96 * j + 48 * c : 96 * j + 48 * c + 48, 128 * i : 128 * i + 128] for c in range(2)], 1
                        )
                        for i in range(2)
                    ],
                    0,
                )
                res.append(times2(x, z_out[pl.ds(256 * j, 256)]))
            tiles = (res[0][:, :128], res[0][:, 128:] + res[1][:, :128], res[1][:, 128:])
            for i in range(2):
                for t in range(3):
                    ob[pl.ds((2 * pair + i) * XROWS + 4 * t + b, PAIRS, stride=12), :] = tiles[t][48 * i : 48 * i + 48]

            @pl.when(b == BANDS - 1)
            def _():
                for i in range(2):
                    store(2 * pair + i).start()

            return carry

        lax.fori_loop(0, OWN // 2, local, 0)
        return carry

    lax.fori_loop(0, BANDS, last, 0)

    @pl.when(grp < OWN)
    def _():
        for d, q in slab_peers:
            send_row(d, q).wait_send()
        for d, q in band_peers:
            send_rows(d, q, grp).wait_send()

    out_hart.wait()
    for d, q in slab_peers:
        send_pot(d, q).wait_send()
        for a in range(3):
            send_share(a, d, q).wait_send()
            send_tail(a, d, q).wait_send()
            send_head(a, d, q).wait_send()
    for d, q in band_peers:
        for a in range(3):
            send_part(a, d, q).wait_send()
        send_modes(d, q).wait_send()

    def drain(b, carry):
        for d, q in slab_peers:
            send_line(b, d, q).wait_send()
            send_back(b + 1, d, q).wait_send()
        return carry

    lax.fori_loop(0, BANDS - 1, drain, 0)
    for i in range(OWN):
        store(i).wait()


def body(orbitals, potential):
    rows = orbitals.reshape(BANDS, OWN, XROWS // BANDS, 128).transpose(1, 2, 0, 3).reshape(OWN * XROWS, 128)
    t = tables()
    consts = [jnp.asarray(t[name]) for name in NAMES]
    vmem = lambda *shape: pltpu.VMEM(shape, F32)
    dma = lambda *shape: pltpu.SemaphoreType.DMA(shape)
    ev, har = pl.pallas_call(
        kernel,
        out_shape=(
            jax.ShapeDtypeStruct((OWN * XROWS, 128), F32),
            jax.ShapeDtypeStruct(potential.shape, F32),
        ),
        in_specs=[pl.BlockSpec(memory_space=pl.ANY)] * (2 + len(consts)),
        out_specs=[pl.BlockSpec(memory_space=pl.ANY)] * 2,
        scratch_shapes=[pltpu.VMEM(c.shape, c.dtype) for c in consts]
        + [
            vmem(OWN * XROWS, 128),
            vmem(BANDS * BAND, 128),
            vmem(BANDS * BAND, 128),
            vmem(BANDS, 2 * GRID, LINE),
            vmem(BANDS * BAND, 128),
            vmem(BANDS * BAND, 128),
            vmem(OWN * XROWS, 128),
            vmem(GRID, LINE),
            vmem(128, LINE),
            vmem(GROUPS, 8, LINE),
            vmem(8, LINE),
            vmem(8, LINE),
            vmem(SLABS, 8, LINE),
            vmem(768, 128),
            vmem(GRID, 1024),
            vmem(128, LINE),
            vmem(GRID, LINE),
            vmem(SLABS, OWN, LINE),
            vmem(GRID, LINE),
            vmem(GRID, LINE),
            vmem(GRID, LINE),
            vmem(GRID * 16, 128),
            vmem(OWN * SLABS * 16, 128),
            vmem(OWN, GRID * GRID),
            dma(OWN), dma(OWN),
            dma(SLABS), dma(SLABS),
            dma(BANDS, SLABS), dma(BANDS, SLABS),
            dma(BANDS, SLABS), dma(BANDS, SLABS),
            dma(3, GROUPS), dma(3, GROUPS),
            dma(3, SLABS), dma(3, SLABS),
            dma(GROUPS), dma(GROUPS),
            dma(SLABS), dma(SLABS),
            dma(GROUPS), dma(GROUPS),
            dma(BANDS + 1),
            dma(len(consts)),
            dma(3, SLABS), dma(3, SLABS),
            dma(3, SLABS), dma(3, SLABS),
        ],
        compiler_params=pltpu.CompilerParams(
            collective_id=0, has_side_effects=True, vmem_limit_bytes=56 * 1024 * 1024
        ),
    )(rows, potential, *consts)
    return ev.reshape(OWN, XROWS // BANDS, BANDS, 128).transpose(2, 0, 1, 3).reshape(orbitals.shape), har


def solution(mesh):
    return jax.shard_map(
        body,
        mesh=mesh,
        in_specs=(P("band", "slab", None), P("slab", None)),
        out_specs=(P("band", "slab", None), P("slab", None)),
        check_vma=False,
    )
```

time: 143 us -> 127 us (0.89)
  local copies, waits for them, and re-layouts: 13.4 us -> 4.9 us
  Pallas kernels: 129 us -> 122 us
    pallas_call x1, Pallas kernels: 129 us -> 122 us  [body(): pl.pallas_call(kernel, out_shape=(jax.ShapeDtypeStruct((OWN * XROWS, 128)...]
    pallas_call x1 -> x0, local copies, waits for them, and re-layouts: 6.47 us -> none  [body(): pl.pallas_call(kernel, out_shape=(jax.ShapeDtypeStruct(orbitals.shape, F3...]
    unnamed x4, local copies, waits for them, and re-layouts: 6.98 us -> 4.9 us
where the time goes in v1:
time: 127 us
  Pallas kernels  122 us (96%)
  local copies, waits for them, and re-layouts  4.9 us (4%)
    pallas_call x1, Pallas kernels, body(): pl.pallas_call(kernel, out_shape=(jax.ShapeDtypeStruct((OWN * XROWS, 128)...  122 us
    unnamed x4, local copies, waits for them, and re-layouts  4.9 us

profile of v1, /device:TPU:1, one launch (start us, length us, event | category | flops | bytes accessed | tf_op | source)
XLA Modules:
  0.0 127.1 jit_solution(721599893987475431)
XLA Ops:
  0.6 121.6 %shard_map.167 = (f32[6912,128]{1,0:T(8,128)}, f32[12,9216]{1,0:T(8,128)}) custom-call(f32[6912,128]{1,0:T(8,128)} %bitcast.11, f32[12,9216]{1,0:T(8,128)} %pot.1, bf16[512,256]{1,0:T(8,128)(2,1)} %constant.28.clone.refs_0_, bf16[192,192]{1,0:T(8,128)(2,1)} %constant.29.clone.refs_1_, bf16[192,192]{1,0:T(8,128)(2,1)} %constant.30.clone.refs_2_, ...), custom_call_target="tpu_custom_call" | custom-call | tf_op jit(solution)/shard_map/pallas_call | solution.py:681
  122.2 0.0 copy-start
  122.2 4.1 %copy.22 = f32[4,12,18432]{2,0,1:T(4,128)} copy(f32[4,12,18432]{2,0,1:T(4,128)} %bitcast.10) | data formatting | bytes 7077888
  126.3 0.0 copy-done
  126.3 0.8 copy.23
Async XLA Ops:
  122.2 4.1 %copy-start = (f32[12,9216]{1,0:T(8,128)S(1)}, f32[12,9216]{1,0:T(8,128)}, u32[]{:S(2)}) copy-start(f32[12,9216]{1,0:T(8,128)} %get-tuple-element.9) | copy-start | bytes 1327108

commit v2 on v1

--- a/solution.py
+++ b/solution.py
@@ -21,6 +21,8 @@
 TILES = LINE // 128
 BLOCK = TILES * 2 * OWN
 BAND = SLABS * BLOCK
+MODES = 56
+PIECES = ((0, 24), (24, 16), (40, 16))
 XROWS = 2 * GRID * GRID // 128 * BANDS
 PAIRS = GRID // 2
 SHARE = GRID // GROUPS
@@ -113,10 +115,10 @@
     t["y_in"] = exact(ky.transpose(1, 0, 2, 3, 5, 4, 6).reshape(192, 192))
     ky = g[:, pair_y][:, :, :, :, wire_y]
     t["y_out"] = exact(ky.transpose(1, 0, 2, 4, 3, 5, 6).reshape(192, 192))
-    kx = g.reshape(2, GRID, 2, SLABS, OWN)
-    t["x_in"] = exact(kx.transpose(0, 1, 3, 2, 4).reshape(192, 192))
-    kx = g.reshape(2, SLABS, OWN, 2, GRID)
-    t["x_out"] = exact(kx.transpose(1, 0, 2, 3, 4).reshape(192, 192))
+    kx = g.reshape(2, GRID, 2, SLABS, 3, 4)
+    t["x_in"] = exact(kx.transpose(0, 1, 3, 4, 2, 5).reshape(192, 192))
+    kx = g.reshape(2, SLABS, 3, 4, 2, GRID)
+    t["x_out"] = exact(kx.transpose(1, 2, 0, 3, 4, 5).reshape(192, 192))
     q, ksq = real_basis()
     qx = np.zeros((GROUPS, 8, GRID))
     qx[:, :SHARE] = q.reshape(GROUPS, SHARE, GRID)
@@ -220,9 +222,9 @@
     consts, refs = refs[: len(NAMES)], refs[len(NAMES) :]
     z_in, y_in, x_in, kxz, ky2, qx, qz, qy, qyt, qzt, qxt, x_out, y_out, z_out = consts
     (
-     ib, wire, lines, moved, back, home, ob, dens, dq, part, share, modes, whole, zt, green, hq, hart,
-           vb, vl, cosb, sinb, hs, hrow, harv,
-           in_sem, out_sem, pot_s, pot_r, w_s, w_r, b_s, b_r, rs_s, rs_r, ag_s, ag_r, hq_s, hq_r, h_s, h_r, g_s, g_r, own_sem, const_sem, tail_s, tail_r, head_s, head_r) = refs
+     ib, wire, lines, moved, back, home, dens, dq, part, share, modes, whole, zt, green, hq, hart,
+           vb, vl, cosb, sinb, hs, hrow,
+           in_sem, pot_s, pot_r, w_s, w_r, b_s, b_r, rs_s, rs_r, ag_s, ag_r, hq_s, hq_r, h_s, h_r, g_s, g_r, own_sem, const_sem, tail_s, tail_r, head_s, head_r, first_s, first_r, last_s, last_r) = refs
     me = lax.axis_index("slab")
     grp = lax.axis_index("band")
     slab_peers = [(d, lax.rem(me + d, SLABS)) for d in range(1, SLABS)]
@@ -255,6 +257,21 @@
 
     def band_copy(src, dst, s, r, q):
         return pltpu.make_async_remote_copy(src, dst, s, r, device_id={"band": q}, device_id_type=MESH)
+
+    def row_of(pair):
+        return pair // 2 * 8 + lax.rem(pair, 2) * 2
+
+    def quad(ref, b, q, k):
+        return ref.reshape(BANDS * SLABS * TILES, 24, 128).at[pl.ds((b * SLABS + q) * TILES, TILES), pl.ds(pl.multiple_of(8 * k, 8), 8)]
+
+    def quad_copy(src, dst, b, k, d, q, send, recv):
+        return slab_copy(quad(src, b, q, k), quad(dst, b, me, k), send.at[k, d], recv.at[k, d], q)
+
+    def send_first(k, d, q):
+        return quad_copy(wire, lines, 0, k, d, q, first_s, first_r)
+
+    def send_last(k, d, q):
+        return quad_copy(back, home, BANDS - 1, k, d, q, last_s, last_r)
 
     def first(b, carry):
         def local(pair, carry):
@@ -288,16 +305,22 @@
                 tiles = packed([r[48 * j : 48 * j + 48, 128 * i : 128 * i + 128] for j in range(4)])
                 for t in range(3):
                     for c in range(2):
-                        wire[pl.ds(b * BAND + t * 24 + c * OWN + x, 24, stride=72), :] = tiles[t][24 * c : 24 * c + 24]
+                        wire[pl.ds(b * BAND + t * 24 + 4 * c + row_of(pair) + i, 24, stride=72), :] = tiles[t][24 * c : 24 * c + 24]
+
+            @pl.when((b == 0) & (pair == 1))
+            def _():
+                pl.semaphore_wait(barrier, SLABS - 1 + GROUPS - 1)
+
+            @pl.when((b == 0) & (lax.rem(pair, 2) == 1))
+            def _():
+                for d, q in slab_peers:
+                    send_first(pair // 2, d, q).start()
+
             return carry
 
         lax.fori_loop(0, OWN // 2, local, 0)
 
-        @pl.when(b == 0)
-        def _():
-            pl.semaphore_wait(barrier, SLABS - 1 + GROUPS - 1)
-
-        @pl.when(b < BANDS - 1)
+        @pl.when((b > 0) & (b < BANDS - 1))
         def _():
             for d, q in slab_peers:
                 send_line(b, d, q).start()
@@ -374,8 +397,17 @@
 
     def lines_x(b, carry):
         own_line(b).wait()
-        for d, q in slab_peers:
-            send_line(b, d, q).wait_recv()
+
+        @pl.when(b == 0)
+        def _():
+            for k in range(3):
+                for d, q in slab_peers:
+                    send_first(k, d, q).wait_recv()
+
+        @pl.when(b > 0)
+        def _():
+            for d, q in slab_peers:
+                send_line(b, d, q).wait_recv()
 
         def chunk(a, carry):
             kx_in(b, a)
@@ -451,16 +483,23 @@
     for a in range(3):
         tiles = packed([zt[pl.ds(4 * a + j, 8, stride=16), :] for j in range(4)])
         for t in range(3):
-            modes[:, 384 * a + 128 * t : 384 * a + 128 * t + 128] = tiles[t]
-
-    def send_modes(d, q):
-        return band_copy(modes, hq.at[pl.ds(pl.multiple_of(grp * 8, 8), 8)], hq_s.at[d], hq_r.at[d], q)
-
-    for d, q in band_peers:
-        send_modes(d, q).start()
-    hq[pl.ds(pl.multiple_of(grp * 8, 8), 8)] = modes[...]
-    for d, q in band_peers:
-        send_modes(d, q).wait_recv()
+            modes[SHARE * (3 * a + t) : SHARE * (3 * a + t) + 8, :] = tiles[t]
+
+    def send_modes(k, d, q):
+        start, rows = PIECES[k]
+        return band_copy(
+            modes.at[pl.ds(start, rows)],
+            hq.at[pl.ds(grp * MODES + start, rows)],
+            hq_s.at[k, d],
+            hq_r.at[k, d],
+            q,
+        )
+
+    for k in range(3):
+        for d, q in band_peers:
+            send_modes(k, d, q).start()
+    hq[pl.ds(pl.multiple_of(grp * MODES, 8), MODES)] = modes[...]
+
     def send_back(b, d, q):
         return slab_copy(
             back.at[pl.ds(b * BAND + q * BLOCK, BLOCK)],
@@ -495,9 +534,24 @@
             for t in range(3):
                 back[pl.ds(b * BAND + q * BLOCK + (3 * a + t) * 24, 24)] = r[24 * q : 24 * q + 24, 128 * t : 128 * t + 128]
 
-    def head(a, carry):
-        at = pl.ds(pl.multiple_of(a * 384, 128), 384)
-        h = left(qxt[pl.ds(0, GRID)], qxt[pl.ds(GRID, GRID)], hq[:, at])
+    for a in range(3):
+        for d, q in band_peers:
+            send_modes(a, d, q).wait_recv()
+        at = pl.ds(384 * a, 384)
+        x = jnp.concatenate(
+            [
+                jnp.concatenate(
+                    [
+                        hq[MODES * g + SHARE * (3 * a + t) : MODES * g + SHARE * (3 * a + t) + 8, :]
+                        for g in range(GROUPS)
+                    ],
+                    0,
+                )
+                for t in range(3)
+            ],
+            1,
+        )
+        h = left(qxt[pl.ds(0, GRID)], qxt[pl.ds(GRID, GRID)], x)
         hart[:, at] = h
         s, c = sin_cos((vl[:, at] + h) * TIME_STEP)
         sinb[:, at] = s * SCALE**6
@@ -505,9 +559,6 @@
         kx_out(0, a)
         for d, q in slab_peers:
             send_head(a, d, q).start()
-        return carry
-
-    lax.fori_loop(0, 3, head, 0)
     own_back(0).start()
 
     for t in range(TILES):
@@ -542,16 +593,21 @@
             return carry
 
         lax.fori_loop(0, 3, chunk, 0)
-        for d, q in slab_peers:
-            send_back(b, d, q).start()
+        @pl.when(b < BANDS - 1)
+        def _():
+            for d, q in slab_peers:
+                send_back(b, d, q).start()
+
+        @pl.when(b == BANDS - 1)
+        def _():
+            for k in range(3):
+                for d, q in slab_peers:
+                    send_last(k, d, q).start()
+
         own_back(b).start()
         return carry
 
     lax.fori_loop(1, BANDS, kick, 0)
-
-    def store(i):
-        at = pl.ds(i * XROWS, XROWS)
-        return pltpu.make_async_copy(ob.at[at], ev.at[at], out_sem.at[i])
 
     def rows_out():
         @pl.when(grp < OWN)
@@ -572,12 +628,9 @@
 
         for s in range(SLABS):
             for t in range(TILES):
-                harv[:, LINE * s + 128 * t : LINE * s + 128 * t + 128] = hrow[
+                har[:, LINE * s + 128 * t : LINE * s + 128 * t + 128] = hrow[
                     pl.ds(16 * s + t, OWN, stride=SLABS * 16), :
                 ]
-        out_hart.start()
-
-    out_hart = pltpu.make_async_copy(harv, har, own_sem.at[BANDS])
 
     def last(b, carry):
         @pl.when(b == 1)
@@ -596,18 +649,23 @@
                 for d, q in slab_peers:
                     send_head(a, d, q).wait_recv()
 
-        @pl.when(b > 0)
+        @pl.when((b > 0) & (b < BANDS - 1))
         def _():
             for d, q in slab_peers:
                 send_back(b, d, q).wait_recv()
 
         def local(pair, carry):
+            @pl.when((b == BANDS - 1) & (lax.rem(pair, 2) == 0))
+            def _():
+                for d, q in slab_peers:
+                    send_last(pair // 2, d, q).wait_recv()
+
             cols = []
             for i in range(2):
                 x = 2 * pair + i
                 tiles = [
                     jnp.concatenate(
-                        [home[pl.ds(b * BAND + t * 24 + c * OWN + x, 24, stride=72), :] for c in range(2)], 0
+                        [home[pl.ds(b * BAND + t * 24 + 4 * c + row_of(pair) + i, 24, stride=72), :] for c in range(2)], 0
                     )
                     for t in range(3)
                 ]
@@ -628,12 +686,7 @@
             tiles = (res[0][:, :128], res[0][:, 128:] + res[1][:, :128], res[1][:, 128:])
             for i in range(2):
                 for t in range(3):
-                    ob[pl.ds((2 * pair + i) * XROWS + 4 * t + b, PAIRS, stride=12), :] = tiles[t][48 * i : 48 * i + 48]
-
-            @pl.when(b == BANDS - 1)
-            def _():
-                for i in range(2):
-                    store(2 * pair + i).start()
+                    ev[pl.ds((2 * pair + i) * XROWS + 4 * t + b, PAIRS, stride=12), :] = tiles[t][48 * i : 48 * i + 48]
 
             return carry
 
@@ -649,27 +702,38 @@
         for d, q in band_peers:
             send_rows(d, q, grp).wait_send()
 
-    out_hart.wait()
     for d, q in slab_peers:
         send_pot(d, q).wait_send()
         for a in range(3):
             send_share(a, d, q).wait_send()
             send_tail(a, d, q).wait_send()
             send_head(a, d, q).wait_send()
+            send_first(a, d, q).wait_send()
+            send_last(a, d, q).wait_send()
     for d, q in band_peers:
         for a in range(3):
             send_part(a, d, q).wait_send()
-        send_modes(d, q).wait_send()
+            send_modes(a, d, q).wait_send()
 
     def drain(b, carry):
         for d, q in slab_peers:
             send_line(b, d, q).wait_send()
-            send_back(b + 1, d, q).wait_send()
+            send_back(b, d, q).wait_send()
         return carry
 
-    lax.fori_loop(0, BANDS - 1, drain, 0)
-    for i in range(OWN):
-        store(i).wait()
+    lax.fori_loop(1, BANDS - 1, drain, 0)
+
+
+def result(ev, har, ev_out, har_out, sem):
+    n = ev.shape[0] // 8
+    copies = [
+        pltpu.make_async_copy(ev.at[pl.ds(n * i, n)], ev_out.at[pl.ds(n * i, n)], sem.at[i]) for i in range(8)
+    ]
+    copies.append(pltpu.make_async_copy(har, har_out, sem.at[8]))
+    for copy in copies:
+        copy.start()
+    for copy in copies:
+        copy.wait()
 
 
 def body(orbitals, potential):
@@ -681,11 +745,11 @@
     ev, har = pl.pallas_call(
         kernel,
         out_shape=(
-            jax.ShapeDtypeStruct((OWN * XROWS, 128), F32),
-            jax.ShapeDtypeStruct(potential.shape, F32),
+            pltpu.VMEM((OWN * XROWS, 128), F32),
+            pltpu.VMEM(potential.shape, F32),
         ),
         in_specs=[pl.BlockSpec(memory_space=pl.ANY)] * (2 + len(consts)),
-        out_specs=[pl.BlockSpec(memory_space=pl.ANY)] * 2,
+        out_specs=[pl.BlockSpec(memory_space=pltpu.VMEM)] * 2,
         scratch_shapes=[pltpu.VMEM(c.shape, c.dtype) for c in consts]
         + [
             vmem(OWN * XROWS, 128),
@@ -694,16 +758,15 @@
             vmem(BANDS, 2 * GRID, LINE),
             vmem(BANDS * BAND, 128),
             vmem(BANDS * BAND, 128),
-            vmem(OWN * XROWS, 128),
             vmem(GRID, LINE),
             vmem(128, LINE),
             vmem(GROUPS, 8, LINE),
             vmem(8, LINE),
-            vmem(8, LINE),
+            vmem(MODES, 128),
             vmem(SLABS, 8, LINE),
             vmem(768, 128),
             vmem(GRID, 1024),
-            vmem(128, LINE),
+            vmem(GROUPS * MODES, 128),
             vmem(GRID, LINE),
             vmem(SLABS, OWN, LINE),
             vmem(GRID, LINE),
@@ -711,25 +774,34 @@
             vmem(GRID, LINE),
             vmem(GRID * 16, 128),
             vmem(OWN * SLABS * 16, 128),
-            vmem(OWN, GRID * GRID),
-            dma(OWN), dma(OWN),
+            dma(OWN),
             dma(SLABS), dma(SLABS),
             dma(BANDS, SLABS), dma(BANDS, SLABS),
             dma(BANDS, SLABS), dma(BANDS, SLABS),
             dma(3, GROUPS), dma(3, GROUPS),
             dma(3, SLABS), dma(3, SLABS),
-            dma(GROUPS), dma(GROUPS),
+            dma(3, GROUPS), dma(3, GROUPS),
             dma(SLABS), dma(SLABS),
             dma(GROUPS), dma(GROUPS),
             dma(BANDS + 1),
             dma(len(consts)),
             dma(3, SLABS), dma(3, SLABS),
             dma(3, SLABS), dma(3, SLABS),
+            dma(3, SLABS), dma(3, SLABS),
+            dma(3, SLABS), dma(3, SLABS),
         ],
         compiler_params=pltpu.CompilerParams(
-            collective_id=0, has_side_effects=True, vmem_limit_bytes=56 * 1024 * 1024
+            collective_id=0, has_side_effects=True, vmem_limit_bytes=60416 * 1024
         ),
     )(rows, potential, *consts)
+    ev, har = pl.pallas_call(
+        result,
+        out_shape=(jax.ShapeDtypeStruct(ev.shape, F32), jax.ShapeDtypeStruct(har.shape, F32)),
+        in_specs=[pl.BlockSpec(memory_space=pltpu.VMEM)] * 2,
+        out_specs=[pl.BlockSpec(memory_space=pl.ANY)] * 2,
+        scratch_shapes=[pltpu.SemaphoreType.DMA((9,))],
+        compiler_params=pltpu.CompilerParams(vmem_limit_bytes=1024 * 1024),
+    )(ev, har)
     return ev.reshape(OWN, XROWS // BANDS, BANDS, 128).transpose(2, 0, 1, 3).reshape(orbitals.shape), har
 
 

time: 127 us -> 118 us (0.929)
  Pallas kernels: 122 us -> 117 us
  local copies, waits for them, and re-layouts: 4.9 us -> 0 us
    unnamed x4 -> x0, local copies, waits for them, and re-layouts: 4.9 us -> none
    pallas_call x1 -> x2, Pallas kernels: 122 us -> 117 us  [the longest x1 115 us: body(): pl.pallas_call(kernel, out_shape=(pltpu.VMEM((OWN * XROWS, 128), F32), pl...]
where the time goes in v2:
time: 118 us
  Pallas kernels  117 us (99%)
    pallas_call x1, Pallas kernels, body(): pl.pallas_call(kernel, out_shape=(pltpu.VMEM((OWN * XROWS, 128), F32), pl...  115 us

profile of v2, /device:TPU:1, one launch (start us, length us, event | category | flops | bytes accessed | tf_op | source)
XLA Modules:
  0.0 117.9 jit_solution(14550451258802450406)
XLA Ops:
  0.6 115.2 %shard_map.167 = (f32[6912,128]{1,0:T(8,128)S(1)}, f32[12,9216]{1,0:T(8,128)S(1)}) custom-call(f32[6912,128]{1,0:T(8,128)} %bitcast.10, f32[12,9216]{1,0:T(8,128)} %pot.1, bf16[512,256]{1,0:T(8,128)(2,1)} %constant.28.clone.refs_0_, bf16[192,192]{1,0:T(8,128)(2,1)} %constant.29.clone.refs_1_, bf16[192,192]{1,0:T(8,128)(2,1)} %constant.30.clone.refs_2_, ...), custom_call_target="tpu_custom_call" | custom-call | tf_op jit(solution)/shard_map/pallas_call | solution.py:745
  115.9 2.1 %shard_map.168 = (f32[6912,128]{1,0:T(8,128)}, f32[12,9216]{1,0:T(8,128)}) custom-call(f32[6912,128]{1,0:T(8,128)S(1)} %get-tuple-element.6.ev, f32[12,9216]{1,0:T(8,128)S(1)} %get-tuple-element.7.har), custom_call_target="tpu_custom_call" | custom-call | tf_op jit(solution)/shard_map/pallas_call | solution.py:797

commit v3 on v2

--- a/solution.py
+++ b/solution.py
@@ -237,7 +237,7 @@
         pl.semaphore_signal(barrier, inc=1, device_id={"band": q}, device_id_type=MESH)
 
     def load(i):
-        at = pl.ds(i * XROWS, XROWS)
+        at = pl.ds(i * 2 * XROWS, 2 * XROWS)
         return pltpu.make_async_copy(orb.at[at], ib.at[at], in_sem.at[i])
 
     def table(i):
@@ -245,7 +245,7 @@
 
     table(0).start()
     table(1).start()
-    for i in range(OWN):
+    for i in range(OWN // 2):
         load(i).start()
     for i in range(2, len(NAMES)):
         table(i).start()
@@ -265,20 +265,27 @@
         return ref.reshape(BANDS * SLABS * TILES, 24, 128).at[pl.ds((b * SLABS + q) * TILES, TILES), pl.ds(pl.multiple_of(8 * k, 8), 8)]
 
     def quad_copy(src, dst, b, k, d, q, send, recv):
-        return slab_copy(quad(src, b, q, k), quad(dst, b, me, k), send.at[k, d], recv.at[k, d], q)
+        return slab_copy(quad(src, b, q, k), quad(dst, b, me, k), send.at[k], recv.at[k], q)
 
     def send_first(k, d, q):
         return quad_copy(wire, lines, 0, k, d, q, first_s, first_r)
 
     def send_last(k, d, q):
         return quad_copy(back, home, BANDS - 1, k, d, q, last_s, last_r)
+
+    def done(view, sem):
+        pltpu.make_async_copy(view, view, sem).wait()
+
+    def rows(ref, n):
+        return ref.at[pl.ds(0, n)]
+
+    OTHERS, REST = SLABS - 1, GROUPS - 1
 
     def first(b, carry):
         def local(pair, carry):
             @pl.when(b == 0)
             def _():
-                for i in range(2):
-                    load(2 * pair + i).wait()
+                load(pair).wait()
 
             tiles = [
                 jnp.concatenate(
@@ -338,8 +345,8 @@
         return slab_copy(
             wire.at[pl.ds((BANDS - 1) * BAND + q * BLOCK + 72 * a, 72)],
             lines.at[pl.ds((BANDS - 1) * BAND + me * BLOCK + 72 * a, 72)],
-            tail_s.at[a, d],
-            tail_r.at[a, d],
+            tail_s.at[a],
+            tail_r.at[a],
             q,
         )
 
@@ -347,8 +354,8 @@
         return slab_copy(
             wire.at[pl.ds(b * BAND + q * BLOCK, BLOCK)],
             lines.at[pl.ds(b * BAND + me * BLOCK, BLOCK)],
-            w_s.at[b, d],
-            w_r.at[b, d],
+            w_s.at[b],
+            w_r.at[b],
             q,
         )
 
@@ -360,7 +367,7 @@
 
     def send_pot(d, q):
         return slab_copy(
-            pot.at[:, pl.ds(pl.multiple_of(q * LINE, 128), LINE)], vb.at[me], pot_s.at[d], pot_r.at[d], q
+            pot.at[:, pl.ds(pl.multiple_of(q * LINE, 128), LINE)], vb.at[me], pot_s.at[0], pot_r.at[0], q
         )
 
     for d, q in slab_peers:
@@ -401,13 +408,11 @@
         @pl.when(b == 0)
         def _():
             for k in range(3):
-                for d, q in slab_peers:
-                    send_first(k, d, q).wait_recv()
+                done(rows(lines, OTHERS * 72), first_r.at[k])
 
         @pl.when(b > 0)
         def _():
-            for d, q in slab_peers:
-                send_line(b, d, q).wait_recv()
+            done(rows(lines, OTHERS * BLOCK), w_r.at[b])
 
         def chunk(a, carry):
             kx_in(b, a)
@@ -420,13 +425,12 @@
 
     def send_part(a, d, q):
         at = pl.ds(pl.multiple_of(a * 384, 128), 384)
-        return band_copy(dq.at[pl.ds(pl.multiple_of(q * 8, 8), 8), at], part.at[grp, :, at], rs_s.at[a, d], rs_r.at[a, d], q)
+        return band_copy(dq.at[pl.ds(pl.multiple_of(q * 8, 8), 8), at], part.at[grp, :, at], rs_s.at[a], rs_r.at[a], q)
 
     own_line(BANDS - 1).wait()
 
     def last_lines(a, carry):
-        for d, q in slab_peers:
-            send_tail(a, d, q).wait_recv()
+        done(rows(lines, OTHERS * 72), tail_r.at[a])
         kx_in(BANDS - 1, a)
         at = pl.ds(pl.multiple_of(a * 384, 128), 384)
         dq[:, at] = left(qx[pl.ds(0, 128)], qx[pl.ds(128, 128)], dens[:, at])
@@ -437,19 +441,17 @@
     lax.fori_loop(0, 3, last_lines, 0)
 
     own_pot.wait()
-    for d, q in slab_peers:
-        send_pot(d, q).wait_recv()
+    done(rows(vb, OTHERS), pot_r.at[0])
     for s in range(SLABS):
         vl[OWN * s : OWN * s + OWN, :] = vb[s]
 
     def send_share(a, d, q):
         at = pl.ds(pl.multiple_of(a * 384, 128), 384)
-        return slab_copy(share.at[:, at], whole.at[me, :, at], ag_s.at[a, d], ag_r.at[a, d], q)
+        return slab_copy(share.at[:, at], whole.at[me, :, at], ag_s.at[a], ag_r.at[a], q)
 
     def sums(a, carry):
         at = pl.ds(pl.multiple_of(a * 384, 128), 384)
-        for d, q in band_peers:
-            send_part(a, d, q).wait_recv()
+        done(part.at[pl.ds(0, REST), :, at], rs_r.at[a])
         total = dq[pl.ds(pl.multiple_of(grp * 8, 8), 8), at]
         for d, q in band_peers:
             total = total + part[q, :, at]
@@ -462,8 +464,7 @@
     lax.fori_loop(0, 3, sums, 0)
 
     def along_z(a, carry):
-        for d, q in slab_peers:
-            send_share(a, d, q).wait_recv()
+        done(whole.at[pl.ds(0, OTHERS), :, pl.ds(pl.multiple_of(a * 384, 128), 384)], ag_r.at[a])
         tiles = [
             jnp.concatenate(
                 [whole[s, :, pl.ds(pl.multiple_of(384 * a + 128 * t, 128), 128)] for s in range(SLABS)], 0
@@ -490,8 +491,8 @@
         return band_copy(
             modes.at[pl.ds(start, rows)],
             hq.at[pl.ds(grp * MODES + start, rows)],
-            hq_s.at[k, d],
-            hq_r.at[k, d],
+            hq_s.at[k],
+            hq_r.at[k],
             q,
         )
 
@@ -504,8 +505,8 @@
         return slab_copy(
             back.at[pl.ds(b * BAND + q * BLOCK, BLOCK)],
             home.at[pl.ds(b * BAND + me * BLOCK, BLOCK)],
-            b_s.at[b, d],
-            b_r.at[b, d],
+            b_s.at[b],
+            b_r.at[b],
             q,
         )
 
@@ -517,8 +518,8 @@
         return slab_copy(
             back.at[pl.ds(q * BLOCK + 72 * a, 72)],
             home.at[pl.ds(me * BLOCK + 72 * a, 72)],
-            head_s.at[a, d],
-            head_r.at[a, d],
+            head_s.at[a],
+            head_r.at[a],
             q,
         )
 
@@ -535,8 +536,7 @@
                 back[pl.ds(b * BAND + q * BLOCK + (3 * a + t) * 24, 24)] = r[24 * q : 24 * q + 24, 128 * t : 128 * t + 128]
 
     for a in range(3):
-        for d, q in band_peers:
-            send_modes(a, d, q).wait_recv()
+        done(rows(hq, REST * PIECES[a][1]), hq_r.at[a])
         at = pl.ds(384 * a, 384)
         x = jnp.concatenate(
             [
@@ -568,8 +568,8 @@
         return slab_copy(
             hs.at[pl.ds((q * OWN + grp) * 16, 16)],
             hrow.at[pl.ds((grp * SLABS + me) * 16, 16)],
-            h_s.at[d],
-            h_r.at[d],
+            h_s.at[0],
+            h_r.at[0],
             q,
         )
 
@@ -579,7 +579,7 @@
 
     def send_rows(d, q, g):
         at = pl.ds(g * (SLABS * 16), SLABS * 16)
-        return band_copy(hrow.at[at], hrow.at[at], g_s.at[d], g_r.at[d], q)
+        return band_copy(hrow.at[at], hrow.at[at], g_s.at[0], g_r.at[0], q)
 
     @pl.when(grp < OWN)
     def _():
@@ -613,18 +613,18 @@
         @pl.when(grp < OWN)
         def _():
             own_row.wait()
-            for d, q in slab_peers:
-                send_row(d, q).wait_recv()
+            done(rows(hrow, OTHERS * 16), h_r.at[0])
             for d, q in band_peers:
                 send_rows(d, q, grp).start()
 
     def rows_in():
-        for d, _ in band_peers:
-            source = lax.rem(grp + GROUPS - d, GROUPS)
-
-            @pl.when(source < OWN)
-            def _():
-                send_rows(d, source, source).wait_recv()
+        @pl.when(grp < OWN)
+        def _():
+            done(rows(hrow, (OWN - 1) * SLABS * 16), g_r.at[0])
+
+        @pl.when(grp >= OWN)
+        def _():
+            done(rows(hrow, OWN * SLABS * 16), g_r.at[0])
 
         for s in range(SLABS):
             for t in range(TILES):
@@ -646,19 +646,16 @@
         @pl.when(b == 0)
         def _():
             for a in range(3):
-                for d, q in slab_peers:
-                    send_head(a, d, q).wait_recv()
+                done(rows(home, OTHERS * 72), head_r.at[a])
 
         @pl.when((b > 0) & (b < BANDS - 1))
         def _():
-            for d, q in slab_peers:
-                send_back(b, d, q).wait_recv()
+            done(rows(home, OTHERS * BLOCK), b_r.at[b])
 
         def local(pair, carry):
             @pl.when((b == BANDS - 1) & (lax.rem(pair, 2) == 0))
             def _():
-                for d, q in slab_peers:
-                    send_last(pair // 2, d, q).wait_recv()
+                done(rows(home, OTHERS * 72), last_r.at[pair // 2])
 
             cols = []
             for i in range(2):
@@ -697,31 +694,21 @@
 
     @pl.when(grp < OWN)
     def _():
-        for d, q in slab_peers:
-            send_row(d, q).wait_send()
-        for d, q in band_peers:
-            send_rows(d, q, grp).wait_send()
-
-    for d, q in slab_peers:
-        send_pot(d, q).wait_send()
-        for a in range(3):
-            send_share(a, d, q).wait_send()
-            send_tail(a, d, q).wait_send()
-            send_head(a, d, q).wait_send()
-            send_first(a, d, q).wait_send()
-            send_last(a, d, q).wait_send()
-    for d, q in band_peers:
-        for a in range(3):
-            send_part(a, d, q).wait_send()
-            send_modes(a, d, q).wait_send()
-
-    def drain(b, carry):
-        for d, q in slab_peers:
-            send_line(b, d, q).wait_send()
-            send_back(b, d, q).wait_send()
-        return carry
-
-    lax.fori_loop(1, BANDS - 1, drain, 0)
+        done(rows(hs, OTHERS * 16), h_s.at[0])
+        done(rows(wire, REST * SLABS * 16), g_s.at[0])
+
+    done(rows(vb, OTHERS), pot_s.at[0])
+    for a in range(3):
+        done(whole.at[pl.ds(0, OTHERS), :, pl.ds(384 * a, 384)], ag_s.at[a])
+        done(part.at[pl.ds(0, REST), :, pl.ds(384 * a, 384)], rs_s.at[a])
+        done(rows(hq, REST * PIECES[a][1]), hq_s.at[a])
+        done(rows(wire, OTHERS * 72), first_s.at[a])
+        done(rows(wire, OTHERS * 72), tail_s.at[a])
+        done(rows(back, OTHERS * 72), head_s.at[a])
+        done(rows(back, OTHERS * 72), last_s.at[a])
+    for b in range(1, BANDS - 1):
+        done(rows(wire, OTHERS * BLOCK), w_s.at[b])
+        done(rows(back, OTHERS * BLOCK), b_s.at[b])
 
 
 def result(ev, har, ev_out, har_out, sem):
@@ -774,21 +761,21 @@
             vmem(GRID, LINE),
             vmem(GRID * 16, 128),
             vmem(OWN * SLABS * 16, 128),
-            dma(OWN),
-            dma(SLABS), dma(SLABS),
-            dma(BANDS, SLABS), dma(BANDS, SLABS),
-            dma(BANDS, SLABS), dma(BANDS, SLABS),
-            dma(3, GROUPS), dma(3, GROUPS),
-            dma(3, SLABS), dma(3, SLABS),
-            dma(3, GROUPS), dma(3, GROUPS),
-            dma(SLABS), dma(SLABS),
-            dma(GROUPS), dma(GROUPS),
+            dma(OWN // 2),
+            dma(1), dma(1),
+            dma(BANDS), dma(BANDS),
+            dma(BANDS), dma(BANDS),
+            dma(3), dma(3),
+            dma(3), dma(3),
+            dma(3), dma(3),
+            dma(1), dma(1),
+            dma(1), dma(1),
             dma(BANDS + 1),
             dma(len(consts)),
-            dma(3, SLABS), dma(3, SLABS),
-            dma(3, SLABS), dma(3, SLABS),
-            dma(3, SLABS), dma(3, SLABS),
-            dma(3, SLABS), dma(3, SLABS),
+            dma(3), dma(3),
+            dma(3), dma(3),
+            dma(3), dma(3),
+            dma(3), dma(3),
         ],
         compiler_params=pltpu.CompilerParams(
             collective_id=0, has_side_effects=True, vmem_limit_bytes=60416 * 1024

time: 118 us -> 113 us (0.958)
  Pallas kernels: 117 us -> 112 us
    pallas_call x1, Pallas kernels: 115 us -> 110 us  [body(): pl.pallas_call(kernel, out_shape=(pltpu.VMEM((OWN * XROWS, 128), F32), pl...]
where the time goes in v3:
time: 113 us
  Pallas kernels  112 us (99%)
    pallas_call x1, Pallas kernels, body(): pl.pallas_call(kernel, out_shape=(pltpu.VMEM((OWN * XROWS, 128), F32), pl...  110 us

profile of v3, /device:TPU:1, one launch (start us, length us, event | category | flops | bytes accessed | tf_op | source)
XLA Modules:
  0.0 112.7 jit_solution(3819584927842946639)
XLA Ops:
  0.6 110.0 %shard_map.167 = (f32[6912,128]{1,0:T(8,128)S(1)}, f32[12,9216]{1,0:T(8,128)S(1)}) custom-call(f32[6912,128]{1,0:T(8,128)} %bitcast.10, f32[12,9216]{1,0:T(8,128)} %pot.1, bf16[512,256]{1,0:T(8,128)(2,1)} %constant.28.clone.refs_0_, bf16[192,192]{1,0:T(8,128)(2,1)} %constant.29.clone.refs_1_, bf16[192,192]{1,0:T(8,128)(2,1)} %constant.30.clone.refs_2_, ...), custom_call_target="tpu_custom_call" | custom-call | tf_op jit(solution)/shard_map/pallas_call | solution.py:732
  110.7 2.1 %shard_map.168 = (f32[6912,128]{1,0:T(8,128)}, f32[12,9216]{1,0:T(8,128)}) custom-call(f32[6912,128]{1,0:T(8,128)S(1)} %get-tuple-element.6.ev, f32[12,9216]{1,0:T(8,128)S(1)} %get-tuple-element.7.har), custom_call_target="tpu_custom_call" | custom-call | tf_op jit(solution)/shard_map/pallas_call | solution.py:784

commit v4 on v3

--- a/solution.py
+++ b/solution.py
@@ -26,7 +26,8 @@
 XROWS = 2 * GRID * GRID // 128 * BANDS
 PAIRS = GRID // 2
 SHARE = GRID // GROUPS
-SCALE = 1.88474
+SCALE, TURN = 1.2310180561521498, 4.856431605497022
+OFFSET = math.remainder(6 * TURN, 2 * math.pi)
 F32 = jnp.float32
 BF16 = jnp.bfloat16
 
@@ -35,7 +36,7 @@
     n = np.arange(GRID)
     m = (n + GRID // 2) % GRID - GRID // 2
     k = 2.0 * math.pi / GRID * m
-    phase = np.exp(-1j * k * k * TIME_STEP / 4)
+    phase = np.exp(1j * (TURN - k * k * TIME_STEP / 4))
     exact = np.fft.ifft(phase) / SCALE
     line = np.stack([exact.real, exact.imag]).astype(np.float32).astype(ml_dtypes.bfloat16).astype(np.float64)
 
@@ -224,11 +225,20 @@
     (
      ib, wire, lines, moved, back, home, dens, dq, part, share, modes, whole, zt, green, hq, hart,
            vb, vl, cosb, sinb, hs, hrow,
-           in_sem, pot_s, pot_r, w_s, w_r, b_s, b_r, rs_s, rs_r, ag_s, ag_r, hq_s, hq_r, h_s, h_r, g_s, g_r, own_sem, const_sem, tail_s, tail_r, head_s, head_r, first_s, first_r, last_s, last_r) = refs
+           in_sem, pot_s, pot_r, w_s, w_r, b_s, b_r, rs_s, rs_r, ag_s, ag_r, hq_s, hq_r, h_s, h_r, g_s, g_r, own_sem, const_sem, tail_r, head_r, first_r, last_r) = refs
     me = lax.axis_index("slab")
     grp = lax.axis_index("band")
-    slab_peers = [(d, lax.rem(me + d, SLABS)) for d in range(1, SLABS)]
-    band_peers = [(d, lax.rem(grp + d, GROUPS)) for d in range(1, GROUPS)]
+    slab_peers = [
+        (2 * i + j, lax.rem(me // 2 + i, 4) * 2 + lax.rem(me + j, 2))
+        for i, j in ((2, 0), (2, 1), (1, 0), (3, 0), (1, 1), (3, 1), (0, 1))
+    ]
+    offsets = sorted(
+        [(i, j) for i in range(4) for j in range(4) if i or j],
+        key=lambda o: -min(o[0], 4 - o[0]) - min(o[1], 4 - o[1]),
+    )
+    band_peers = [
+        (4 * i + j, lax.rem(grp // 4 + i, 4) * 4 + lax.rem(lax.rem(grp, 4) + j, 4)) for i, j in offsets
+    ]
 
     barrier = pltpu.get_barrier_semaphore()
     for _, q in slab_peers:
@@ -265,13 +275,13 @@
         return ref.reshape(BANDS * SLABS * TILES, 24, 128).at[pl.ds((b * SLABS + q) * TILES, TILES), pl.ds(pl.multiple_of(8 * k, 8), 8)]
 
     def quad_copy(src, dst, b, k, d, q, send, recv):
-        return slab_copy(quad(src, b, q, k), quad(dst, b, me, k), send.at[k], recv.at[k], q)
+        return slab_copy(quad(src, b, q, k), quad(dst, b, me, k), send.at[0], recv.at[k], q)
 
     def send_first(k, d, q):
-        return quad_copy(wire, lines, 0, k, d, q, first_s, first_r)
+        return quad_copy(wire, lines, 0, k, d, q, w_s, first_r)
 
     def send_last(k, d, q):
-        return quad_copy(back, home, BANDS - 1, k, d, q, last_s, last_r)
+        return quad_copy(back, home, BANDS - 1, k, d, q, b_s, last_r)
 
     def done(view, sem):
         pltpu.make_async_copy(view, view, sem).wait()
@@ -345,7 +355,7 @@
         return slab_copy(
             wire.at[pl.ds((BANDS - 1) * BAND + q * BLOCK + 72 * a, 72)],
             lines.at[pl.ds((BANDS - 1) * BAND + me * BLOCK + 72 * a, 72)],
-            tail_s.at[a],
+            w_s.at[0],
             tail_r.at[a],
             q,
         )
@@ -354,7 +364,7 @@
         return slab_copy(
             wire.at[pl.ds(b * BAND + q * BLOCK, BLOCK)],
             lines.at[pl.ds(b * BAND + me * BLOCK, BLOCK)],
-            w_s.at[b],
+            w_s.at[0],
             w_r.at[b],
             q,
         )
@@ -425,7 +435,7 @@
 
     def send_part(a, d, q):
         at = pl.ds(pl.multiple_of(a * 384, 128), 384)
-        return band_copy(dq.at[pl.ds(pl.multiple_of(q * 8, 8), 8), at], part.at[grp, :, at], rs_s.at[a], rs_r.at[a], q)
+        return band_copy(dq.at[pl.ds(pl.multiple_of(q * 8, 8), 8), at], part.at[grp, :, at], rs_s.at[0], rs_r.at[a], q)
 
     own_line(BANDS - 1).wait()
 
@@ -447,7 +457,7 @@
 
     def send_share(a, d, q):
         at = pl.ds(pl.multiple_of(a * 384, 128), 384)
-        return slab_copy(share.at[:, at], whole.at[me, :, at], ag_s.at[a], ag_r.at[a], q)
+        return slab_copy(share.at[:, at], whole.at[me, :, at], ag_s.at[0], ag_r.at[a], q)
 
     def sums(a, carry):
         at = pl.ds(pl.multiple_of(a * 384, 128), 384)
@@ -491,7 +501,7 @@
         return band_copy(
             modes.at[pl.ds(start, rows)],
             hq.at[pl.ds(grp * MODES + start, rows)],
-            hq_s.at[k],
+            hq_s.at[0],
             hq_r.at[k],
             q,
         )
@@ -505,7 +515,7 @@
         return slab_copy(
             back.at[pl.ds(b * BAND + q * BLOCK, BLOCK)],
             home.at[pl.ds(b * BAND + me * BLOCK, BLOCK)],
-            b_s.at[b],
+            b_s.at[0],
             b_r.at[b],
             q,
         )
@@ -518,7 +528,7 @@
         return slab_copy(
             back.at[pl.ds(q * BLOCK + 72 * a, 72)],
             home.at[pl.ds(me * BLOCK + 72 * a, 72)],
-            head_s.at[a],
+            b_s.at[0],
             head_r.at[a],
             q,
         )
@@ -553,7 +563,7 @@
         )
         h = left(qxt[pl.ds(0, GRID)], qxt[pl.ds(GRID, GRID)], x)
         hart[:, at] = h
-        s, c = sin_cos((vl[:, at] + h) * TIME_STEP)
+        s, c = sin_cos((vl[:, at] + h) * TIME_STEP + OFFSET)
         sinb[:, at] = s * SCALE**6
         cosb[:, at] = c * SCALE**6
         kx_out(0, a)
@@ -698,17 +708,11 @@
         done(rows(wire, REST * SLABS * 16), g_s.at[0])
 
     done(rows(vb, OTHERS), pot_s.at[0])
-    for a in range(3):
-        done(whole.at[pl.ds(0, OTHERS), :, pl.ds(384 * a, 384)], ag_s.at[a])
-        done(part.at[pl.ds(0, REST), :, pl.ds(384 * a, 384)], rs_s.at[a])
-        done(rows(hq, REST * PIECES[a][1]), hq_s.at[a])
-        done(rows(wire, OTHERS * 72), first_s.at[a])
-        done(rows(wire, OTHERS * 72), tail_s.at[a])
-        done(rows(back, OTHERS * 72), head_s.at[a])
-        done(rows(back, OTHERS * 72), last_s.at[a])
-    for b in range(1, BANDS - 1):
-        done(rows(wire, OTHERS * BLOCK), w_s.at[b])
-        done(rows(back, OTHERS * BLOCK), b_s.at[b])
+    done(rows(wire, 3 * OTHERS * 24), ag_s.at[0])
+    done(rows(wire, 3 * REST * 24), rs_s.at[0])
+    done(rows(wire, REST * MODES), hq_s.at[0])
+    done(rows(wire, BANDS * OTHERS * BLOCK), w_s.at[0])
+    done(rows(back, BANDS * OTHERS * BLOCK), b_s.at[0])
 
 
 def result(ev, har, ev_out, har_out, sem):
@@ -763,19 +767,16 @@
             vmem(OWN * SLABS * 16, 128),
             dma(OWN // 2),
             dma(1), dma(1),
-            dma(BANDS), dma(BANDS),
-            dma(BANDS), dma(BANDS),
-            dma(3), dma(3),
-            dma(3), dma(3),
-            dma(3), dma(3),
+            dma(1), dma(BANDS),
+            dma(1), dma(BANDS),
+            dma(1), dma(3),
+            dma(1), dma(3),
+            dma(1), dma(3),
             dma(1), dma(1),
             dma(1), dma(1),
             dma(BANDS + 1),
             dma(len(consts)),
-            dma(3), dma(3),
-            dma(3), dma(3),
-            dma(3), dma(3),
-            dma(3), dma(3),
+            dma(3), dma(3), dma(3), dma(3),
         ],
         compiler_params=pltpu.CompilerParams(
             collective_id=0, has_side_effects=True, vmem_limit_bytes=60416 * 1024

time: 113 us -> 112 us (level)
  no operation moved by 1% of the time
where the time goes in v4:
time: 112 us
  Pallas kernels  111 us (99%)
    pallas_call x1, Pallas kernels, body(): pl.pallas_call(kernel, out_shape=(pltpu.VMEM((OWN * XROWS, 128), F32), pl...  109 us

profile of v4, /device:TPU:1, one launch (start us, length us, event | category | flops | bytes accessed | tf_op | source)
XLA Modules:
  0.0 111.9 jit_solution(18369835056574494028)
XLA Ops:
  0.6 109.2 %shard_map.167 = (f32[6912,128]{1,0:T(8,128)S(1)}, f32[12,9216]{1,0:T(8,128)S(1)}) custom-call(f32[6912,128]{1,0:T(8,128)} %bitcast.10, f32[12,9216]{1,0:T(8,128)} %pot.1, bf16[512,256]{1,0:T(8,128)(2,1)} %constant.28.clone.refs_0_, bf16[192,192]{1,0:T(8,128)(2,1)} %constant.29.clone.refs_1_, bf16[192,192]{1,0:T(8,128)(2,1)} %constant.30.clone.refs_2_, ...), custom_call_target="tpu_custom_call" | custom-call | tf_op jit(solution)/shard_map/pallas_call | solution.py:736
  109.8 2.1 %shard_map.168 = (f32[6912,128]{1,0:T(8,128)}, f32[12,9216]{1,0:T(8,128)}) custom-call(f32[6912,128]{1,0:T(8,128)S(1)} %get-tuple-element.6.ev, f32[12,9216]{1,0:T(8,128)S(1)} %get-tuple-element.7.har), custom_call_target="tpu_custom_call" | custom-call | tf_op jit(solution)/shard_map/pallas_call | solution.py:785

commit v5 on v4

--- a/solution.py
+++ b/solution.py
@@ -21,8 +21,10 @@
 TILES = LINE // 128
 BLOCK = TILES * 2 * OWN
 BAND = SLABS * BLOCK
+CHUNKS = ((0, 4), (4, 3), (7, 2))
 MODES = 56
-PIECES = ((0, 24), (24, 16), (40, 16))
+PIECES = ((0, 16), (16, 16), (32, 24))
+HEADS = ((0, 2), (2, 3), (5, 4))
 XROWS = 2 * GRID * GRID // 128 * BANDS
 PAIRS = GRID // 2
 SHARE = GRID // GROUPS
@@ -353,8 +355,8 @@
 
     def send_tail(a, d, q):
         return slab_copy(
-            wire.at[pl.ds((BANDS - 1) * BAND + q * BLOCK + 72 * a, 72)],
-            lines.at[pl.ds((BANDS - 1) * BAND + me * BLOCK + 72 * a, 72)],
+            wire.at[pl.ds((BANDS - 1) * BAND + q * BLOCK + 24 * CHUNKS[a][0], 24 * CHUNKS[a][1])],
+            lines.at[pl.ds((BANDS - 1) * BAND + me * BLOCK + 24 * CHUNKS[a][0], 24 * CHUNKS[a][1])],
             w_s.at[0],
             tail_r.at[a],
             q,
@@ -397,18 +399,18 @@
 
     dens[...] = jnp.zeros_like(dens)
 
-    def kx_in(b, a):
+    def kx_in(b, start, count):
         x = jnp.concatenate(
             [
                 jnp.concatenate(
-                    [lines[pl.ds(b * BAND + s * BLOCK + (3 * a + t) * 24, 24)] for s in range(SLABS)], 0
+                    [lines[pl.ds(b * BAND + s * BLOCK + (start + t) * 24, 24)] for s in range(SLABS)], 0
                 )
-                for t in range(3)
+                for t in range(count)
             ],
             1,
         )
         r = left2(x_in[...], x)
-        at = pl.ds(pl.multiple_of(a * 384, 128), 384)
+        at = pl.ds(pl.multiple_of(start * 128, 128), 128 * count)
         moved[b, :, at] = r
         dens[:, at] += r[:GRID] * r[:GRID] + r[GRID:] * r[GRID:]
 
@@ -425,7 +427,7 @@
             done(rows(lines, OTHERS * BLOCK), w_r.at[b])
 
         def chunk(a, carry):
-            kx_in(b, a)
+            kx_in(b, 3 * a, 3)
             return carry
 
         lax.fori_loop(0, 3, chunk, 0)
@@ -433,22 +435,22 @@
 
     lax.fori_loop(0, BANDS - 1, lines_x, 0)
 
+    def lanes(a):
+        return pl.ds(128 * CHUNKS[a][0], 128 * CHUNKS[a][1])
+
     def send_part(a, d, q):
-        at = pl.ds(pl.multiple_of(a * 384, 128), 384)
+        at = lanes(a)
         return band_copy(dq.at[pl.ds(pl.multiple_of(q * 8, 8), 8), at], part.at[grp, :, at], rs_s.at[0], rs_r.at[a], q)
 
     own_line(BANDS - 1).wait()
 
-    def last_lines(a, carry):
-        done(rows(lines, OTHERS * 72), tail_r.at[a])
-        kx_in(BANDS - 1, a)
-        at = pl.ds(pl.multiple_of(a * 384, 128), 384)
+    for a in range(3):
+        done(rows(lines, OTHERS * 24 * CHUNKS[a][1]), tail_r.at[a])
+        kx_in(BANDS - 1, *CHUNKS[a])
+        at = lanes(a)
         dq[:, at] = left(qx[pl.ds(0, 128)], qx[pl.ds(128, 128)], dens[:, at])
         for d, q in band_peers:
             send_part(a, d, q).start()
-        return carry
-
-    lax.fori_loop(0, 3, last_lines, 0)
 
     own_pot.wait()
     done(rows(vb, OTHERS), pot_r.at[0])
@@ -456,11 +458,11 @@
         vl[OWN * s : OWN * s + OWN, :] = vb[s]
 
     def send_share(a, d, q):
-        at = pl.ds(pl.multiple_of(a * 384, 128), 384)
+        at = lanes(a)
         return slab_copy(share.at[:, at], whole.at[me, :, at], ag_s.at[0], ag_r.at[a], q)
 
-    def sums(a, carry):
-        at = pl.ds(pl.multiple_of(a * 384, 128), 384)
+    for a in range(3):
+        at = lanes(a)
         done(part.at[pl.ds(0, REST), :, at], rs_r.at[a])
         total = dq[pl.ds(pl.multiple_of(grp * 8, 8), 8), at]
         for d, q in band_peers:
@@ -469,23 +471,17 @@
         for d, q in slab_peers:
             send_share(a, d, q).start()
         whole[me, :, at] = total
-        return carry
-
-    lax.fori_loop(0, 3, sums, 0)
-
-    def along_z(a, carry):
-        done(whole.at[pl.ds(0, OTHERS), :, pl.ds(pl.multiple_of(a * 384, 128), 384)], ag_r.at[a])
+
+    for a in range(3):
+        done(whole.at[pl.ds(0, OTHERS), :, lanes(a)], ag_r.at[a])
         tiles = [
             jnp.concatenate(
-                [whole[s, :, pl.ds(pl.multiple_of(384 * a + 128 * t, 128), 128)] for s in range(SLABS)], 0
+                [whole[s, :, 384 * a + 128 * t : 384 * a + 128 * t + 128] for s in range(SLABS)], 0
             )
             for t in range(3)
         ]
         x = jnp.concatenate(unpacked(tiles), 0)
-        zt[pl.ds(pl.multiple_of(256 * a, 256), 256)] = times(x, qz[pl.ds(0, 128)], qz[pl.ds(128, 128)])
-        return carry
-
-    lax.fori_loop(0, 3, along_z, 0)
+        zt[pl.ds(256 * a, 256)] = times(x, qz[pl.ds(0, 128)], qz[pl.ds(128, 128)])
     x = jnp.concatenate([zt[pl.ds(i, GRID, stride=8), :] for i in range(8)], 1)
     x = left(qy[pl.ds(0, GRID)], qy[pl.ds(GRID, GRID)], x) * green[...]
     x = left(qyt[me, 0:16], qyt[me, 16:32], x)
@@ -526,15 +522,15 @@
 
     def send_head(a, d, q):
         return slab_copy(
-            back.at[pl.ds(q * BLOCK + 72 * a, 72)],
-            home.at[pl.ds(me * BLOCK + 72 * a, 72)],
+            back.at[pl.ds(q * BLOCK + 24 * HEADS[a][0], 24 * HEADS[a][1])],
+            home.at[pl.ds(me * BLOCK + 24 * HEADS[a][0], 24 * HEADS[a][1])],
             b_s.at[0],
             head_r.at[a],
             q,
         )
 
-    def kx_out(b, a):
-        at = pl.ds(pl.multiple_of(a * 384, 128), 384)
+    def kx_out(b, start, count):
+        at = pl.ds(pl.multiple_of(start * 128, 128), 128 * count)
         re = moved[b, 0:GRID, at]
         im = moved[b, GRID : 2 * GRID, at]
         cs = cosb[:, at]
@@ -542,22 +538,22 @@
         x = jnp.concatenate([re * cs + im * sn, im * cs - re * sn], 0)
         r = left2(x_out[...], x)
         for q in range(SLABS):
-            for t in range(3):
-                back[pl.ds(b * BAND + q * BLOCK + (3 * a + t) * 24, 24)] = r[24 * q : 24 * q + 24, 128 * t : 128 * t + 128]
+            for t in range(count):
+                back[pl.ds(b * BAND + q * BLOCK + (start + t) * 24, 24)] = r[24 * q : 24 * q + 24, 128 * t : 128 * t + 128]
 
     for a in range(3):
         done(rows(hq, REST * PIECES[a][1]), hq_r.at[a])
-        at = pl.ds(384 * a, 384)
+        at = pl.ds(128 * HEADS[a][0], 128 * HEADS[a][1])
         x = jnp.concatenate(
             [
                 jnp.concatenate(
                     [
-                        hq[MODES * g + SHARE * (3 * a + t) : MODES * g + SHARE * (3 * a + t) + 8, :]
+                        hq[MODES * g + SHARE * t : MODES * g + SHARE * t + 8, :]
                         for g in range(GROUPS)
                     ],
                     0,
                 )
-                for t in range(3)
+                for t in range(HEADS[a][0], sum(HEADS[a]))
             ],
             1,
         )
@@ -566,7 +562,7 @@
         s, c = sin_cos((vl[:, at] + h) * TIME_STEP + OFFSET)
         sinb[:, at] = s * SCALE**6
         cosb[:, at] = c * SCALE**6
-        kx_out(0, a)
+        kx_out(0, *HEADS[a])
         for d, q in slab_peers:
             send_head(a, d, q).start()
     own_back(0).start()
@@ -599,7 +595,7 @@
 
     def kick(b, carry):
         def chunk(a, carry):
-            kx_out(b, a)
+            kx_out(b, 3 * a, 3)
             return carry
 
         lax.fori_loop(0, 3, chunk, 0)
@@ -656,7 +652,7 @@
         @pl.when(b == 0)
         def _():
             for a in range(3):
-                done(rows(home, OTHERS * 72), head_r.at[a])
+                done(rows(home, OTHERS * 24 * HEADS[a][1]), head_r.at[a])
 
         @pl.when((b > 0) & (b < BANDS - 1))
         def _():

time: 112 us -> 112 us (level)
  no operation moved by 1% of the time
where the time goes in v5:
time: 112 us
  Pallas kernels  111 us (99%)
    pallas_call x1, Pallas kernels, body(): pl.pallas_call(kernel, out_shape=(pltpu.VMEM((OWN * XROWS, 128), F32), pl...  109 us

profile of v5, /device:TPU:1, one launch (start us, length us, event | category | flops | bytes accessed | tf_op | source)
XLA Modules:
  0.0 111.6 jit_solution(12280105646204759717)
XLA Ops:
  0.6 108.9 %shard_map.167 = (f32[6912,128]{1,0:T(8,128)S(1)}, f32[12,9216]{1,0:T(8,128)S(1)}) custom-call(f32[6912,128]{1,0:T(8,128)} %bitcast.10, f32[12,9216]{1,0:T(8,128)} %pot.1, bf16[512,256]{1,0:T(8,128)(2,1)} %constant.28.clone.refs_0_, bf16[192,192]{1,0:T(8,128)(2,1)} %constant.29.clone.refs_1_, bf16[192,192]{1,0:T(8,128)(2,1)} %constant.30.clone.refs_2_, ...), custom_call_target="tpu_custom_call" | custom-call | tf_op jit(solution)/shard_map/pallas_call | solution.py:732
  109.5 2.1 %shard_map.168 = (f32[6912,128]{1,0:T(8,128)}, f32[12,9216]{1,0:T(8,128)}) custom-call(f32[6912,128]{1,0:T(8,128)S(1)} %get-tuple-element.6.ev, f32[12,9216]{1,0:T(8,128)S(1)} %get-tuple-element.7.har), custom_call_target="tpu_custom_call" | custom-call | tf_op jit(solution)/shard_map/pallas_call | solution.py:781
